TPU v7x, 32 devices: a whole 2x2x4 slice. The times are simulated.
32 devices in a mesh: sec: 4 (over x, core), key: 8 (over z, y).
Axes of the slice: x: 2, y: 2, z: 4, core: 2. Of those that a mesh axis runs over, the one named last changes fastest.
Arguments:
- query: bfloat16 [4096, 16, 128], P(('sec', 'key')), may hold values from -64 to 64
- key: bfloat16 [4096, 4, 128], P(('sec', 'key')), may hold values from -5 to 5
- value: bfloat16 [4096, 4, 128], P(('sec', 'key')), may hold values from -5 to 5
- raw_directions: bfloat16 [4096, 4, 128], P(('sec', 'key')), may hold values from -5 to 5
- beta_raw_logits: float32 [4096, 4], P(('sec', 'key')), may hold values from -7 to 7
Outputs:
- attended: bfloat16 [4096, 16, 128], P(('sec', 'key'))
All inputs are finite; a program needn't handle non-finite values.
Results may differ from a plain program's by a relative error of at most 0.0055.
Values sent between devices are 32-bit elements; how exact they have to be, the bound alone decides.
No kernel may reach another device: no remote copies, remote signals or barrier semaphores. Data moves between devices by JAX's collectives and lax.ppermute only.
A program may use at most 64 MiB of HBM per device.

v0:
```python
import functools

import jax
import jax.numpy as jnp
from jax import lax
from jax.experimental import pallas as pl
from jax.experimental.pallas import tpu as pltpu
from jax.sharding import PartitionSpec as P


F32 = jnp.float32
BF16 = jnp.bfloat16
VMEM_LIMIT = 20 * 1024 * 1024
LOW = -1e30
LOG2_E = 1.4426950408889634


def halves(x):
    h = x.astype(BF16)
    return h, (x - h.astype(F32)).astype(BF16)


def left_cat(x):
    h, l = halves(x)
    return jnp.concatenate([h, l, h], axis=1)


def right_rows(x):
    h, l = halves(x)
    return jnp.concatenate([h, h, l], axis=0)


def mm(a, b):
    return lax.dot_general(a, b, (((1,), (0,)), ((), ())), preferred_element_type=F32)


def dot_nn(a, b):
    return mm(left_cat(a), right_rows(b))


def call(kernel, out_shape, args, scratch=(), scalars=None, flops=0, nbytes=0, exps=0):
    vm = pl.BlockSpec(memory_space=pltpu.VMEM)
    sm = pl.BlockSpec(memory_space=pltpu.SMEM)
    specs = [vm] * len(args)
    if scalars is not None:
        specs = [sm] + specs
        args = [scalars] + list(args)
    outs = jax.tree.map(lambda _: vm, out_shape)
    return pl.pallas_call(
        kernel,
        out_shape=out_shape,
        in_specs=specs,
        out_specs=outs,
        scratch_shapes=list(scratch),
        compiler_params=pltpu.CompilerParams(vmem_limit_bytes=VMEM_LIMIT),
        cost_estimate=pl.CostEstimate(flops=flops, bytes_accessed=nbytes, transcendentals=exps),
    )(*args)


def ident(n):
    rows = lax.broadcasted_iota(jnp.int32, (n, n), 0)
    return (rows == lax.broadcasted_iota(jnp.int32, (n, n), 1)).astype(F32)


def block_kernel(heads, length, width, scal, *refs):
    packs = refs[:heads]
    km_ref, wk_ref, yz_ref = refs[heads:]
    place = scal[0]
    rows = lax.broadcasted_iota(jnp.int32, (length, length), 0)
    cols = lax.broadcasted_iota(jnp.int32, (length, length), 1)
    eye = ident(length)
    strict = rows > cols
    units, turned, betas, lows, xs = [], [], [], [], []
    for d in range(heads):
        w = packs[d][length : 2 * length]
        b_row = packs[d][2 * length : 2 * length + 1]
        beta = 2.0 / (1.0 + jnp.exp(-b_row))
        beta = jnp.transpose(jnp.broadcast_to(beta, (length, length)))
        unit = w / jnp.sqrt(jnp.sum(w * w, -1, keepdims=True) + 1e-06)
        across = jnp.transpose(unit)
        low = jnp.where(strict, beta * dot_nn(unit, across), 0.0)
        units.append(unit)
        turned.append(across)
        betas.append(beta)
        lows.append(low)
        level = (rows // 2 == cols // 2) & (rows % 2 == 1) & (cols % 2 == 0)
        xs.append(eye - jnp.where(level, low, 0.0))
    size = 2
    while size < length:
        level = (
            (rows // (2 * size) == cols // (2 * size))
            & ((rows // size) % 2 == 1)
            & ((cols // size) % 2 == 0)
        )
        part = [dot_nn(jnp.where(level, lows[d], 0.0), xs[d]) for d in range(heads)]
        part = [dot_nn(xs[d], part[d]) for d in range(heads)]
        xs = [xs[d] - part[d] for d in range(heads)]
        size *= 2
    for d in range(heads):
        slot = lax.rem(place - d + heads, heads)
        unit, beta, across = units[d], betas[d], turned[d]
        kt = jnp.transpose(packs[d][0:length])
        kb = kt.astype(BF16)
        uh, ul = halves(unit)
        cross = mm(jnp.concatenate([uh, ul], axis=1), jnp.concatenate([kb, kb], axis=0))
        cross = jnp.where(strict, cross, 0.0)
        zy = dot_nn(xs[d], jnp.concatenate([beta * cross, beta[:, :width] * unit], axis=1))
        base = jnp.concatenate([kt, ident(width)], axis=1)
        km_ref[slot] = base - dot_nn(across, zy)
        ah, al = halves(across)
        wk_ref[slot] = jnp.concatenate(
            [
                jnp.concatenate([ah, kb], axis=1),
                jnp.concatenate([al, jnp.zeros_like(kb)], axis=1),
            ],
            axis=0,
        )
        yz_ref[slot] = right_rows(zy)


def section_kernel(heads, ring, length, scal, *refs):
    kms = refs[:ring]
    kmcat_ref, pack_ref = refs[ring:]
    low = scal[1]
    width = pack_ref.shape[0]
    blocks = heads * ring
    for r in range(ring):
        lane = lax.rem(low - r + ring, ring)
        for t in range(heads):
            kmcat_ref[t * ring + lane] = right_rows(kms[r][t])
    suffix = ident(width)
    for b in range(blocks - 1, -1, -1):
        got = mm(left_cat(suffix), kmcat_ref[b])
        pack_ref[:, b * length : (b + 1) * length] = got[:, :length]
        suffix = got[:, length:]
    pack_ref[:, blocks * length :] = suffix


def value_kernel(heads, ring, length, scal, *refs):
    vs = refs[:ring]
    vb_ref, vsec_ref = refs[ring:]
    for r in range(ring):
        lane = lax.rem(scal[1] - r + ring, ring)
        for d in range(heads):
            b = lax.rem(scal[0] - d + heads, heads) * ring + lane
            at = pl.ds(pl.multiple_of(b * length, length), length)
            vb_ref[at] = vs[r][d].astype(BF16)
            vsec_ref[at] = vs[r][d]


def near_kernel(heads, ring, length, width, scal, *refs):
    qs = refs[:heads]
    wk_ref, yz_ref, kmcat_ref, vb_ref = refs[heads : heads + 4]
    qcat_ref, ml_ref, acc_ref = refs[heads + 4 : heads + 7]
    q_s, s_s = refs[heads + 7 :]
    place, low = scal[0], scal[1]
    rows = qs[0].shape[0]
    scale = width ** (-0.5) * LOG2_E
    blocks = heads * ring
    keys = blocks * length
    token = lax.rem(lax.broadcasted_iota(jnp.int32, (rows, length), 0), length)
    causal = token >= lax.broadcasted_iota(jnp.int32, (rows, length), 1)
    lane_id = lax.broadcasted_iota(jnp.int32, (rows // 2, 128), 1)
    for d in range(heads):
        q_s[d] = qs[d][...]

    def at(b):
        return pl.ds(pl.multiple_of(b * length, length), length)

    def piece(d, carry):
        t = lax.rem(place - d + heads, heads)
        b_own = t * ring + low
        qf = q_s[d]
        q = qf.astype(BF16)
        both = mm(jnp.concatenate([q, q], axis=1), wk_ref[t])
        qw = jnp.where(causal, both[:, :length], 0.0)
        u = mm(left_cat(qw), yz_ref[t])
        q_s[d] = (qf - u[:, length:]) * scale
        s_s[:, at(b_own)] = jnp.where(causal, (both[:, length:] - u[:, :length]) * scale, LOW)

        def clear(b, c):
            s_s[:, at(b)] = jnp.full((rows, length), LOW, F32)
            return c

        lax.fori_loop(b_own + 1, blocks, clear, 0)

        def step(i, c):
            b = b_own - 1 - i
            both = mm(left_cat(q_s[d]), kmcat_ref[b])
            s_s[:, at(b)] = both[:, :length]
            q_s[d] = both[:, length:]
            return c

        lax.fori_loop(0, b_own, step, 0)
        qcat_ref[d] = left_cat(q_s[d])

        def finish(n):
            for half in range(2):
                part = slice(half * rows // 2, (half + 1) * rows // 2)
                s = s_s[part, :n]
                top = jnp.max(s, -1, keepdims=True)
                p = jnp.exp2(s - top)
                ml_ref[d, part] = jnp.where(lane_id < 64, top, jnp.sum(p, -1, keepdims=True))
                acc_ref[d, part] = mm(p.astype(BF16), vb_ref[:n])

        small = b_own < blocks // 2

        @pl.when(small)
        def _():
            finish(keys // 2)

        @pl.when(jnp.logical_not(small))
        def _():
            finish(keys)

        return carry

    lax.fori_loop(0, heads, piece, 0)


def prep_kernel(hops, scal, *refs):
    n = 2 * hops + 1
    packs, values = refs[:n], refs[n : 2 * n]
    kc_ref, vc_ref, got = refs[2 * n :]
    sec = scal[2]
    core = lax.rem(sec, 2)
    width = got.shape[0]
    keys = got.shape[1] - width
    got_map = ident(width)

    def take(dst, i):
        dst[...] = packs[i][...]

    def take_v(dist, i):
        vc_ref[dist - 1] = values[i][...].astype(BF16)

    for dist in range(1, n + 1):
        p = dist // 2
        if dist % 2 == 0:
            take(got, 2 * p - 1)
            take_v(dist, 2 * p - 1)
        else:

            @pl.when(core == 1)
            def _():
                take(got, 2 * p)
                take_v(dist, 2 * p)

            if p + 1 <= hops:

                @pl.when(core == 0)
                def _():
                    take(got, 2 * p + 2)
                    take_v(dist, 2 * p + 2)

        moved = mm(left_cat(got_map), right_rows(got[...])) if dist > 1 else got[...]
        kc_ref[dist - 1] = right_rows(moved[:, :keys])
        got_map = moved[:, keys:]


def far_kernel(first, parts, scal, q_ref, ml_ref, acc_ref, k_ref, v_ref, *refs):
    count = len(refs) - 3
    outs = refs[:count]
    m_s, l_s, a_s = refs[count:]
    rows = q_ref.shape[1]
    size = rows // parts
    spots = [(d, p) for d in range(count) for p in range(parts)]
    for i, (d, p) in enumerate(spots):
        part = slice(p * size, (p + 1) * size)
        m_s[i] = ml_ref[first + d, part, 0:1]
        l_s[i] = ml_ref[first + d, part, 64:65]
        a_s[i] = acc_ref[first + d, part]

    def scores(i, sec):
        d, p = spots[i]
        return mm(q_ref[first + d, p * size : (p + 1) * size], k_ref[sec])

    def step(sec, c):
        s = scores(0, sec)
        for i in range(len(spots)):
            coming = scores(i + 1, sec) if i + 1 < len(spots) else None
            old = m_s[i]
            top = jnp.maximum(old, jnp.max(s, -1, keepdims=True))
            p = jnp.exp2(s - top)
            f = jnp.exp2(old - top)
            m_s[i] = top
            l_s[i] = l_s[i] * f + jnp.sum(p, -1, keepdims=True)
            a_s[i] = a_s[i] * f + mm(p.astype(BF16), v_ref[sec])
            s = coming
        return c

    lax.fori_loop(0, jnp.minimum(scal[2], k_ref.shape[0]), step, 0)
    for i, (d, p) in enumerate(spots):
        outs[d][p * size : (p + 1) * size] = a_s[i] / l_s[i]


def join_kernel(heads, scal, *refs):
    out_ref = refs[heads]
    for d in range(heads):
        out_ref[lax.rem(scal[0] + d, heads)] = refs[d][...].astype(BF16)


def steps(query, key, value, raw_directions, beta_raw_logits):
    length, q_count, width = query.shape
    heads = key.shape[1]
    group = q_count // heads
    key_count, sec_count = lax.axis_size("key"), lax.axis_size("sec")
    ring = key_count // heads
    hops = sec_count // 2 - 1
    key_index, sec_index = lax.axis_index("key"), lax.axis_index("sec")
    place, low = key_index // ring, key_index % ring
    scal = jnp.stack([place, low, sec_index]).astype(jnp.int32)
    blocks = heads * ring
    rows = group * length
    keys = blocks * length

    def around(d):
        return [(k, ((k // ring + d) % heads) * ring + k % ring) for k in range(key_count)]

    def across(d):
        return [(k, (k // ring) * ring + (k % ring + d) % ring) for k in range(key_count)]

    def send(x, axis, pairs):
        return lax.ppermute(x, axis, pairs)

    def chunks(x):
        return [
            lax.dynamic_index_in_dim(x, lax.rem(place + d, heads), 0, keepdims=False)
            for d in range(heads)
        ]

    def deal(own):
        return [own[0]] + [send(own[d], "key", around(d)) for d in range(1, heads)]

    def gather(x):
        return [x] + [send(x, "key", across(d)) for d in range(1, ring)]

    def by_head(x):
        return jnp.transpose(x.astype(F32), (1, 0, 2))

    sds = jax.ShapeDtypeStruct
    lines = jnp.transpose(beta_raw_logits, (1, 0))[:, None, :]
    lines = jnp.pad(lines, ((0, 0), (0, 7), (0, 0)))
    pack = jnp.concatenate([by_head(key), by_head(raw_directions), lines], axis=1)
    packs = deal(chunks(pack))
    values = deal(chunks(by_head(value)))
    qs = deal(chunks(by_head(query).reshape(heads, rows, width)))

    km, wk, yz = call(
        functools.partial(block_kernel, heads, length, width),
        (
            sds((heads, width, length + width), F32),
            sds((heads, 2 * width, 2 * length), BF16),
            sds((heads, 3 * length, length + width), BF16),
        ),
        packs,
        scalars=scal,
        flops=heads * 20 * 6 * length**3,
        nbytes=heads * 10 * length * width * 4,
    )

    v_own = jnp.stack(values)

    def arrange(parts):
        return call(
            functools.partial(value_kernel, heads, ring, length),
            (sds((keys, width), BF16), sds((keys, width), F32)),
            parts,
            scalars=scal,
            nbytes=blocks * length * width * 10,
        )

    v_parts = gather(v_own)
    km_parts = gather(km)
    vb, vsec = arrange(v_parts)
    kmcat, packet = call(
        functools.partial(section_kernel, heads, ring, length),
        (
            sds((blocks, 3 * width, length + width), BF16),
            sds((width, blocks * length + width), F32),
        ),
        km_parts,
        scalars=scal,
        flops=blocks * 12 * length**3,
        nbytes=blocks * 8 * length * width * 4,
    )

    pair = [(s, s ^ 1) for s in range(sec_count)]
    rise = [(s, s + 1) for s in range(0, sec_count, 2)]
    v_far = [send(vsec, "sec", rise)]
    k_far = [send(packet, "sec", rise)]
    for p in range(1, hops + 1):
        line = [(s, s + 2 * p) for s in range(sec_count - 2 * p)]
        v_got = arrange(gather(send(v_own, "sec", line)))[1]
        k_got = send(packet, "sec", line)
        v_far += [v_got, send(v_got, "sec", pair)]
        k_far += [k_got, send(k_got, "sec", pair)]
    qcat, ml, acc = call(
        functools.partial(near_kernel, heads, ring, length, width),
        (
            sds((heads, rows, 3 * width), BF16),
            sds((heads, rows, 128), F32),
            sds((heads, rows, width), F32),
        ),
        qs + [wk, yz, kmcat, vb],
        scratch=[pltpu.VMEM((heads, rows, width), F32), pltpu.VMEM((rows, keys), F32)],
        scalars=scal,
        flops=heads * blocks // 2 * rows * width * length * 14,
        nbytes=heads * rows * width * 16,
        exps=heads * blocks // 2 * rows * length,
    )
    far_count = 2 * hops + 1
    kc, vc = call(
        functools.partial(prep_kernel, hops),
        (sds((far_count, 3 * width, keys), BF16), sds((far_count, keys, width), BF16)),
        k_far + v_far,
        scratch=[pltpu.VMEM((width, keys + width), F32)],
        scalars=scal,
        flops=far_count * width * width * keys * 6,
        nbytes=far_count * keys * width * 16,
    )
    parts = 2

    def far(first, count):
        got = call(
            functools.partial(far_kernel, first, parts),
            (sds((rows, width), F32),) * count,
            [qcat, ml, acc, kc, vc],
            scratch=[
                pltpu.VMEM((count * parts, rows // parts, 1), F32),
                pltpu.VMEM((count * parts, rows // parts, 1), F32),
                pltpu.VMEM((count * parts, rows // parts, width), F32),
            ],
            scalars=scal,
            flops=count * rows * far_count * keys * width * 8,
            nbytes=count * rows * width * 20 + far_count * keys * width * 8,
            exps=count * rows * far_count * keys,
        )
        return list(got)

    back = [None] * heads
    for d in [heads // 2] + [d for d in range(1, heads) if d != heads // 2] + [0]:
        (piece,) = far(d, 1)
        back[d] = send(piece, "key", around(-d)) if d else piece
    joined = call(
        functools.partial(join_kernel, heads),
        sds((heads, rows, width), BF16),
        back,
        scalars=scal,
        nbytes=heads * rows * width * 6,
    )
    return jnp.transpose(joined.reshape(q_count, length, width), (1, 0, 2))


def solution(mesh):
    rows = P(("sec", "key"), None, None)
    return jax.shard_map(
        steps,
        mesh=mesh,
        in_specs=(rows, rows, rows, rows, P(("sec", "key"), None)),
        out_specs=rows,
        check_vma=False,
    )
```

profile of v0, /device:TPU:23, one launch (start us, length us, event | category | flops | bytes accessed | tf_op | source)
XLA Modules:
  0.0 118.1 jit_solution(276665161223105319)
XLA Ops:
  2.4 2.4 %collective-permute-start.5 = (f32[264,128]{1,0:T(8,128)S(1)}, f32[264,128]{1,0:T(8,128)S(1)}, u32[]{:S(2)}, u32[]{:S(2)}) collective-permute-start(f32[264,128]{1,0:T(8,128)S(1)} %bitcast.41), channel_id=1, source_target_pairs={{0,6},{1,7},{2,0},{3,1},{4,2},{5,3},{6,4},{7,5},{8,14},{9,15},{10,... | collective-permute-start | bytes 405512 | tf_op jit(solution)/shard_map/ppermute | solution.py:324
  4.9 2.8 %collective-permute-done.4.refs_2_ = f32[264,128]{1,0:T(8,128)S(1)} collective-permute-done((f32[264,128]{1,0:T(8,128)S(1)}, f32[264,128]{1,0:T(8,128)S(1)}, u32[]{:S(2)}, u32[]{:S(2)}) %collective-permute-start.4) | collective-permute-done | bytes 135200 | tf_op jit(solution)/shard_map/ppermute | solution.py:324
  7.7 5.5 %collective-permute-done.5.refs_3_ = f32[264,128]{1,0:T(8,128)S(1)} collective-permute-done((f32[264,128]{1,0:T(8,128)S(1)}, f32[264,128]{1,0:T(8,128)S(1)}, u32[]{:S(2)}, u32[]{:S(2)}) %collective-permute-start.5) | collective-permute-done | bytes 135200 | tf_op jit(solution)/shard_map/ppermute | solution.py:324
  13.2 4.2 %collective-permute-done.3.refs_1_ = f32[264,128]{1,0:T(8,128)S(1)} collective-permute-done((f32[264,128]{1,0:T(8,128)S(1)}, f32[264,128]{1,0:T(8,128)S(1)}, u32[]{:S(2)}, u32[]{:S(2)}) %collective-permute-start.3) | collective-permute-done | bytes 135200 | tf_op jit(solution)/shard_map/ppermute | solution.py:324
  17.5 4.3 %shard_map.55 = (f32[4,128,256]{2,1,0:T(8,128)S(1)}, bf16[4,256,256]{2,1,0:T(8,128)(2,1)S(1)}, bf16[4,384,256]{2,1,0:T(8,128)(2,1)S(1)}) custom-call(s32[3]{0:T(128)S(1)} %pad_add_fusion.scal, f32[264,128]{1,0:T(8,128)S(1)} %bitcast.37, f32[264,128]{1,0:T(8,128)S(1)} %collective-permute-done.3.refs_1_, f32[264,128]{1,0:T(8,128)S(1)} %collective-permute-done.4.refs_2_, ...), custom_call_target="tpu_custom_call" | custom-call | flops 1006632960 | bytes 2621440 | tf_op jit(solution)/shard_map/pallas_call | solution.py:49
  23.9 1.9 %collective-permute-done.9 = f32[128,128]{1,0:T(8,128)S(1)} collective-permute-done((f32[128,128]{1,0:T(8,128)S(1)}, f32[128,128]{1,0:T(8,128)S(1)}, u32[]{:S(2)}, u32[]{:S(2)}) %collective-permute-start.9) | collective-permute-done | bytes 65568 | tf_op jit(solution)/shard_map/ppermute | solution.py:324
  26.8 3.2 %collective-permute-done.7 = f32[128,128]{1,0:T(8,128)S(1)} collective-permute-done((f32[128,128]{1,0:T(8,128)S(1)}, f32[128,128]{1,0:T(8,128)S(1)}, u32[]{:S(2)}, u32[]{:S(2)}) %collective-permute-start.7) | collective-permute-done | bytes 65568 | tf_op jit(solution)/shard_map/ppermute | solution.py:324
  31.4 3.6 %collective-permute-done.6.refs_1_ = f32[4,128,256]{2,1,0:T(8,128)S(1)} collective-permute-done((f32[4,128,256]{2,1,0:T(8,128)S(1)}, f32[4,128,256]{2,1,0:T(8,128)S(1)}, u32[]{:S(2)}, u32[]{:S(2)}) %collective-permute-start.6) | collective-permute-done | bytes 524320 | tf_op jit(solution)/shard_map/ppermute | solution.py:324
  34.9 2.1 %shard_map.56 = (bf16[8,384,256]{2,1,0:T(8,128)(2,1)S(1)}, f32[128,1152]{1,0:T(8,128)S(1)}) custom-call(s32[3]{0:T(128)S(1)} %pad_add_fusion.scal, f32[4,128,256]{2,1,0:T(8,128)S(1)} %get-tuple-element.20.refs_0_, f32[4,128,256]{2,1,0:T(8,128)S(1)} %collective-permute-done.6.refs_1_), custom_call_target="tpu_custom_call" | custom-call | flops 201326592 | bytes 4194304 | tf_op jit(solution)/shard_map/pallas_call | solution.py:49
  40.3 1.4 %collective-permute-start.1 = (f32[512,128]{1,0:T(8,128)S(1)}, f32[512,128]{1,0:T(8,128)S(1)}, u32[]{:S(2)}, u32[]{:S(2)}) collective-permute-start(f32[512,128]{1,0:T(8,128)S(1)} %get-tuple-element.32), channel_id=1, source_target_pairs={{0,4},{1,5},{2,6},{3,7},{4,0},{5,1},{6,2},{7,3},{8,12},{9,13},{10,... | collective-permute-start | bytes 786440 | tf_op jit(solution)/shard_map/ppermute | solution.py:324
  41.7 3.4 %collective-permute-done.10.refs_1_ = f32[4,128,128]{2,1,0:T(8,128)S(1)} collective-permute-done((f32[4,128,128]{2,1,0:T(8,128)S(1)}, f32[4,128,128]{2,1,0:T(8,128)S(1)}, u32[]{:S(2)}, u32[]{:S(2)}) %collective-permute-start.10) | collective-permute-done | bytes 262176 | tf_op jit(solution)/shard_map/ppermute | solution.py:324
  46.3 6.1 %collective-permute-done.12.refs_1_ = f32[128,1152]{1,0:T(8,128)S(1)} collective-permute-done((f32[128,1152]{1,0:T(8,128)S(1)}, f32[128,1152]{1,0:T(8,128)S(1)}, u32[]{:S(2)}, u32[]{:S(2)}) %collective-permute-start.12) | collective-permute-done | bytes 589856 | tf_op jit(solution)/shard_map/ppermute | solution.py:324
  52.5 2.2 %collective-permute-start.13 = (f32[128,1152]{1,0:T(8,128)S(1)}, f32[128,1152]{1,0:T(8,128)S(1)}, u32[]{:S(2)}, u32[]{:S(2)}) collective-permute-start(f32[128,1152]{1,0:T(8,128)S(1)} %collective-permute-done.12.refs_1_), channel_id=1, source_target_pairs={{0,8},{8,0},{16,24},{24,16},{1,9},{9,1},{17,25},{25,17},{2,10},{10... | collective-permute-start | bytes 1769480 | tf_op jit(solution)/shard_map/ppermute | solution.py:324
  59.1 1.8 %collective-permute-start = (f32[512,128]{1,0:T(8,128)S(1)}, f32[512,128]{1,0:T(8,128)S(1)}, u32[]{:S(2)}, u32[]{:S(2)}) collective-permute-start(f32[512,128]{1,0:T(8,128)S(1)} %get-tuple-element.33), channel_id=1, source_target_pairs={{0,2},{1,3},{2,4},{3,5},{4,6},{5,7},{6,0},{7,1},{8,10},{9,11},{10,... | collective-permute-start | bytes 786440 | tf_op jit(solution)/shard_map/ppermute | solution.py:324
  60.9 6.0 %collective-permute-done.refs_1_ = f32[512,128]{1,0:T(8,128)S(1)} collective-permute-done((f32[512,128]{1,0:T(8,128)S(1)}, f32[512,128]{1,0:T(8,128)S(1)}, u32[]{:S(2)}, u32[]{:S(2)}) %collective-permute-start) | collective-permute-done | bytes 262176 | tf_op jit(solution)/shard_map/ppermute | solution.py:324
  66.9 10.2 %shard_map.58 = (bf16[4,512,384]{2,1,0:T(8,128)(2,1)S(1)}, f32[4,512,128]{2,1,0:T(8,128)S(1)}, f32[4,512,128]{2,1,0:T(8,128)S(1)}) custom-call(s32[3]{0:T(128)S(1)} %pad_add_fusion.scal, f32[512,128]{1,0:T(8,128)S(1)} %get-tuple-element.34.refs_0_, f32[512,128]{1,0:T(8,128)S(1)} %collective-permute-done.refs_1_, ...), custom_call_target="tpu_custom_call" | custom-call | flops 1879048192 | bytes 4194304 | tf_op jit(solution)/shard_map/pallas_call | solution.py:49
  77.1 1.4 %shard_map.60 = (bf16[3,384,1024]{2,1,0:T(8,128)(2,1)S(1)}, bf16[3,1024,128]{2,1,0:T(8,128)(2,1)S(1)}) custom-call(s32[3]{0:T(128)S(1)} %pad_add_fusion.scal, f32[128,1152]{1,0:T(8,128)S(1)} %collective-permute-done.11.refs_0_, f32[128,1152]{1,0:T(8,128)S(1)} %collective-permute-done.12.refs_1_, f32[128,1152]{1,0:T(8,128)S(1)} %collective-permute-done.13.refs_2_, ...), custom_call_target="tpu_custom_call" | custom-call | flops 301989888 | bytes 6291456 | tf_op jit(solution)/shard_map/pallas_call | solution.py:49
  78.5 4.4 %shard_map.64 = f32[512,128]{1,0:T(8,128)S(1)} custom-call(s32[3]{0:T(128)S(1)} %pad_add_fusion.scal, bf16[4,512,384]{2,1,0:T(8,128)(2,1)S(1)} %get-tuple-element.23.q_ref, f32[4,512,128]{2,1,0:T(8,128)S(1)} %get-tuple-element.24.ml_ref, f32[4,512,128]{2,1,0:T(8,128)S(1)} %get-tuple-element.25.acc_ref, bf16[3,384,1024]{2,1,0:T(8,128)(2,1)S(1)} %get-tuple-element.29.k_ref, ...), custom_call_target="tpu_custom_call" | custom-call | flops 1610612736 | bytes 4456448 | tf_op jit(solution)/shard_map/pallas_call | solution.py:49
  83.0 4.4 %shard_map.63 = f32[512,128]{1,0:T(8,128)S(1)} custom-call(s32[3]{0:T(128)S(1)} %pad_add_fusion.scal, bf16[4,512,384]{2,1,0:T(8,128)(2,1)S(1)} %get-tuple-element.23.q_ref, f32[4,512,128]{2,1,0:T(8,128)S(1)} %get-tuple-element.24.ml_ref, f32[4,512,128]{2,1,0:T(8,128)S(1)} %get-tuple-element.25.acc_ref, bf16[3,384,1024]{2,1,0:T(8,128)(2,1)S(1)} %get-tuple-element.29.k_ref, ...), custom_call_target="tpu_custom_call" | custom-call | flops 1610612736 | bytes 4456448 | tf_op jit(solution)/shard_map/pallas_call | solution.py:49
  87.4 4.6 %shard_map.62 = f32[512,128]{1,0:T(8,128)S(1)} custom-call(s32[3]{0:T(128)S(1)} %pad_add_fusion.scal, bf16[4,512,384]{2,1,0:T(8,128)(2,1)S(1)} %get-tuple-element.23.q_ref, f32[4,512,128]{2,1,0:T(8,128)S(1)} %get-tuple-element.24.ml_ref, f32[4,512,128]{2,1,0:T(8,128)S(1)} %get-tuple-element.25.acc_ref, bf16[3,384,1024]{2,1,0:T(8,128)(2,1)S(1)} %get-tuple-element.29.k_ref, ...), custom_call_target="tpu_custom_call" | custom-call | flops 1610612736 | bytes 4456448 | tf_op jit(solution)/shard_map/pallas_call | solution.py:49
  92.1 3.4 %collective-permute-start.19 = (f32[512,128]{1,0:T(8,128)S(1)}, f32[512,128]{1,0:T(8,128)S(1)}, u32[]{:S(2)}, u32[]{:S(2)}) collective-permute-start(f32[512,128]{1,0:T(8,128)S(1)} %shard_map.63), channel_id=1, source_target_pairs={{0,4},{1,5},{2,6},{3,7},{4,0},{5,1},{6,2},{7,3},{8,12},{9,13},{10,... | collective-permute-start | bytes 786440 | tf_op jit(solution)/shard_map/ppermute | solution.py:324
  95.5 4.4 %shard_map.61.refs_0_ = f32[512,128]{1,0:T(8,128)S(1)} custom-call(s32[3]{0:T(128)S(1)} %pad_add_fusion.scal, bf16[4,512,384]{2,1,0:T(8,128)(2,1)S(1)} %get-tuple-element.23.q_ref, f32[4,512,128]{2,1,0:T(8,128)S(1)} %get-tuple-element.24.ml_ref, f32[4,512,128]{2,1,0:T(8,128)S(1)} %get-tuple-element.25.acc_ref, ...), custom_call_target="tpu_custom_call" | custom-call | flops 1610612736 | bytes 4456448 | tf_op jit(solution)/shard_map/pallas_call | solution.py:49
  100.4 12.3 %collective-permute-done.19.refs_2_ = f32[512,128]{1,0:T(8,128)S(1)} collective-permute-done((f32[512,128]{1,0:T(8,128)S(1)}, f32[512,128]{1,0:T(8,128)S(1)}, u32[]{:S(2)}, u32[]{:S(2)}) %collective-permute-start.19) | collective-permute-done | bytes 262176 | tf_op jit(solution)/shard_map/ppermute | solution.py:324
  112.7 3.7 %collective-permute-done.20.refs_3_ = f32[512,128]{1,0:T(8,128)S(1)} collective-permute-done((f32[512,128]{1,0:T(8,128)S(1)}, f32[512,128]{1,0:T(8,128)S(1)}, u32[]{:S(2)}, u32[]{:S(2)}) %collective-permute-start.20) | collective-permute-done | bytes 262176 | tf_op jit(solution)/shard_map/ppermute | solution.py:324
  (43 shorter events, 17.9 us)
Async XLA Ops:
  2.3 5.4 %collective-permute-start.4 = (f32[264,128]{1,0:T(8,128)S(1)}, f32[264,128]{1,0:T(8,128)S(1)}, u32[]{:S(2)}, u32[]{:S(2)}) collective-permute-start(f32[264,128]{1,0:T(8,128)S(1)} %bitcast.42), channel_id=1, source_target_pairs={{0,4},{1,5},{2,6},{3,7},{4,0},{5,1},{6,2},{7,3},{8,12},{9,13},{10,... | collective-permute-start | bytes 405512 | tf_op jit(solution)/shard_map/ppermute | solution.py:324
  2.4 10.8 %collective-permute-start.5 = (f32[264,128]{1,0:T(8,128)S(1)}, f32[264,128]{1,0:T(8,128)S(1)}, u32[]{:S(2)}, u32[]{:S(2)}) collective-permute-start(f32[264,128]{1,0:T(8,128)S(1)} %bitcast.41), channel_id=1, source_target_pairs={{0,6},{1,7},{2,0},{3,1},{4,2},{5,3},{6,4},{7,5},{8,14},{9,15},{10,... | collective-permute-start | bytes 405512 | tf_op jit(solution)/shard_map/ppermute | solution.py:324
  4.8 12.7 %collective-permute-start.3 = (f32[264,128]{1,0:T(8,128)S(1)}, f32[264,128]{1,0:T(8,128)S(1)}, u32[]{:S(2)}, u32[]{:S(2)}) collective-permute-start(f32[264,128]{1,0:T(8,128)S(1)} %bitcast.40), channel_id=1, source_target_pairs={{0,2},{1,3},{2,4},{3,5},{4,6},{5,7},{6,0},{7,1},{8,10},{9,11},{10,... | collective-permute-start | bytes 405512 | tf_op jit(solution)/shard_map/ppermute | solution.py:324
  17.5 4.6 %copy-start.1 = (bf16[128,4,128]{2,1,0:T(4,128)(2,1)S(1)}, bf16[128,4,128]{2,1,0:T(4,128)(2,1)}, u32[]{:S(2)}) copy-start(bf16[128,4,128]{2,1,0:T(4,128)(2,1)} %param.7) | copy-start | bytes 393220
  21.9 16.5 %copy-start = (bf16[128,16,128]{2,1,0:T(8,128)(2,1)S(1)}, bf16[128,16,128]{2,1,0:T(8,128)(2,1)}, u32[]{:S(2)}) copy-start(bf16[128,16,128]{2,1,0:T(8,128)(2,1)} %param.5) | copy-start | bytes 1572868
  21.9 13.1 %collective-permute-start.6 = (f32[4,128,256]{2,1,0:T(8,128)S(1)}, f32[4,128,256]{2,1,0:T(8,128)S(1)}, u32[]{:S(2)}, u32[]{:S(2)}) collective-permute-start(f32[4,128,256]{2,1,0:T(8,128)S(1)} %get-tuple-element.20.refs_0_), channel_id=1, source_target_pairs={{0,1},{1,0},{2,3},{3,2},{4,5},{5,4},{6,7},{7,6},{8,9},{9,8},{10,11... | collective-permute-start | bytes 1572872 | tf_op jit(solution)/shard_map/ppermute | solution.py:324
  22.4 3.5 %collective-permute-start.9 = (f32[128,128]{1,0:T(8,128)S(1)}, f32[128,128]{1,0:T(8,128)S(1)}, u32[]{:S(2)}, u32[]{:S(2)}) collective-permute-start(f32[128,128]{1,0:T(8,128)S(1)} %bitcast.47), channel_id=1, source_target_pairs={{0,6},{1,7},{2,0},{3,1},{4,2},{5,3},{6,4},{7,5},{8,14},{9,15},{10,... | collective-permute-start | bytes 196616 | tf_op jit(solution)/shard_map/ppermute | solution.py:324
  22.5 4.3 %collective-permute-start.8 = (f32[128,128]{1,0:T(8,128)S(1)}, f32[128,128]{1,0:T(8,128)S(1)}, u32[]{:S(2)}, u32[]{:S(2)}) collective-permute-start(f32[128,128]{1,0:T(8,128)S(1)} %bitcast.45), channel_id=1, source_target_pairs={{0,4},{1,5},{2,6},{3,7},{4,0},{5,1},{6,2},{7,3},{8,12},{9,13},{10,... | collective-permute-start | bytes 196616 | tf_op jit(solution)/shard_map/ppermute | solution.py:324
  22.9 7.2 %collective-permute-start.7 = (f32[128,128]{1,0:T(8,128)S(1)}, f32[128,128]{1,0:T(8,128)S(1)}, u32[]{:S(2)}, u32[]{:S(2)}) collective-permute-start(f32[128,128]{1,0:T(8,128)S(1)} %bitcast.43), channel_id=1, source_target_pairs={{0,2},{1,3},{2,4},{3,5},{4,6},{5,7},{6,0},{7,1},{8,10},{9,11},{10,... | collective-permute-start | bytes 196616 | tf_op jit(solution)/shard_map/ppermute | solution.py:324
  30.1 8.9 %collective-permute-start.15 = (f32[4,128,128]{2,1,0:T(8,128)S(1)}, f32[4,128,128]{2,1,0:T(8,128)S(1)}, u32[]{:S(2)}, u32[]{:S(2)}) collective-permute-start(f32[4,128,128]{2,1,0:T(8,128)S(1)} %pad_maximum_fusion.refs_0_), channel_id=1, source_target_pairs={{0,16},{8,24},{1,17},{9,25},{2,18},{10,26},{3,19},{11,27},{4,20},{... | collective-permute-start | bytes 786440 | tf_op jit(solution)/shard_map/ppermute | solution.py:324
  37.0 15.4 %collective-permute-start.12 = (f32[128,1152]{1,0:T(8,128)S(1)}, f32[128,1152]{1,0:T(8,128)S(1)}, u32[]{:S(2)}, u32[]{:S(2)}) collective-permute-start(f32[128,1152]{1,0:T(8,128)S(1)} %get-tuple-element.26), channel_id=1, source_target_pairs={{0,16},{8,24},{1,17},{9,25},{2,18},{10,26},{3,19},{11,27},{4,20},{... | collective-permute-start | bytes 1769480 | tf_op jit(solution)/shard_map/ppermute | solution.py:324
  38.5 6.6 %collective-permute-start.10 = (f32[4,128,128]{2,1,0:T(8,128)S(1)}, f32[4,128,128]{2,1,0:T(8,128)S(1)}, u32[]{:S(2)}, u32[]{:S(2)}) collective-permute-start(f32[4,128,128]{2,1,0:T(8,128)S(1)} %pad_maximum_fusion.refs_0_), channel_id=1, source_target_pairs={{0,1},{1,0},{2,3},{3,2},{4,5},{5,4},{6,7},{7,6},{8,9},{9,8},{10,11... | collective-permute-start | bytes 786440 | tf_op jit(solution)/shard_map/ppermute | solution.py:324
  38.9 16.3 %collective-permute-start.16 = (f32[4,128,128]{2,1,0:T(8,128)S(1)}, f32[4,128,128]{2,1,0:T(8,128)S(1)}, u32[]{:S(2)}, u32[]{:S(2)}) collective-permute-start(f32[4,128,128]{2,1,0:T(8,128)S(1)} %collective-permute-done.15.refs_0_), channel_id=1, source_target_pairs={{0,1},{1,0},{2,3},{3,2},{4,5},{5,4},{6,7},{7,6},{8,9},{9,8},{10,11... | collective-permute-start | bytes 786440 | tf_op jit(solution)/shard_map/ppermute | solution.py:324
  40.3 17.6 %collective-permute-start.2 = (f32[512,128]{1,0:T(8,128)S(1)}, f32[512,128]{1,0:T(8,128)S(1)}, u32[]{:S(2)}, u32[]{:S(2)}) collective-permute-start(f32[512,128]{1,0:T(8,128)S(1)} %get-tuple-element.31), channel_id=1, source_target_pairs={{0,6},{1,7},{2,0},{3,1},{4,2},{5,3},{6,4},{7,5},{8,14},{9,15},{10,... | collective-permute-start | bytes 786440 | tf_op jit(solution)/shard_map/ppermute | solution.py:324
  40.3 18.7 %collective-permute-start.1 = (f32[512,128]{1,0:T(8,128)S(1)}, f32[512,128]{1,0:T(8,128)S(1)}, u32[]{:S(2)}, u32[]{:S(2)}) collective-permute-start(f32[512,128]{1,0:T(8,128)S(1)} %get-tuple-element.32), channel_id=1, source_target_pairs={{0,4},{1,5},{2,6},{3,7},{4,0},{5,1},{6,2},{7,3},{8,12},{9,13},{10,... | collective-permute-start | bytes 786440 | tf_op jit(solution)/shard_map/ppermute | solution.py:324
  45.1 32.0 %collective-permute-start.11 = (f32[128,1152]{1,0:T(8,128)S(1)}, f32[128,1152]{1,0:T(8,128)S(1)}, u32[]{:S(2)}, u32[]{:S(2)}) collective-permute-start(f32[128,1152]{1,0:T(8,128)S(1)} %get-tuple-element.26), channel_id=1, source_target_pairs={{0,8},{16,24},{1,9},{17,25},{2,10},{18,26},{3,11},{19,27},{4,12},{... | collective-permute-start | bytes 1769480 | tf_op jit(solution)/shard_map/ppermute | solution.py:324
  52.5 24.6 %collective-permute-start.13 = (f32[128,1152]{1,0:T(8,128)S(1)}, f32[128,1152]{1,0:T(8,128)S(1)}, u32[]{:S(2)}, u32[]{:S(2)}) collective-permute-start(f32[128,1152]{1,0:T(8,128)S(1)} %collective-permute-done.12.refs_1_), channel_id=1, source_target_pairs={{0,8},{8,0},{16,24},{24,16},{1,9},{9,1},{17,25},{25,17},{2,10},{10... | collective-permute-start | bytes 1769480 | tf_op jit(solution)/shard_map/ppermute | solution.py:324
  55.3 21.8 %collective-permute-start.14 = (f32[1024,128]{1,0:T(8,128)S(1)}, f32[1024,128]{1,0:T(8,128)S(1)}, u32[]{:S(2)}, u32[]{:S(2)}) collective-permute-start(f32[1024,128]{1,0:T(8,128)S(1)} %get-tuple-element.27), channel_id=1, source_target_pairs={{0,8},{16,24},{1,9},{17,25},{2,10},{18,26},{3,11},{19,27},{4,12},{... | collective-permute-start | bytes 1572872 | tf_op jit(solution)/shard_map/ppermute | solution.py:324
  57.9 19.2 %collective-permute-start.17 = (f32[1024,128]{1,0:T(8,128)S(1)}, f32[1024,128]{1,0:T(8,128)S(1)}, u32[]{:S(2)}, u32[]{:S(2)}) collective-permute-start(f32[1024,128]{1,0:T(8,128)S(1)} %get-tuple-element.28.refs_4_), channel_id=1, source_target_pairs={{0,8},{8,0},{16,24},{24,16},{1,9},{9,1},{17,25},{25,17},{2,10},{10... | collective-permute-start | bytes 1572872 | tf_op jit(solution)/shard_map/ppermute | solution.py:324
  59.1 7.8 %collective-permute-start = (f32[512,128]{1,0:T(8,128)S(1)}, f32[512,128]{1,0:T(8,128)S(1)}, u32[]{:S(2)}, u32[]{:S(2)}) collective-permute-start(f32[512,128]{1,0:T(8,128)S(1)} %get-tuple-element.33), channel_id=1, source_target_pairs={{0,2},{1,3},{2,4},{3,5},{4,6},{5,7},{6,0},{7,1},{8,10},{9,11},{10,... | collective-permute-start | bytes 786440 | tf_op jit(solution)/shard_map/ppermute | solution.py:324
  92.0 8.4 %collective-permute-start.18 = (f32[512,128]{1,0:T(8,128)S(1)}, f32[512,128]{1,0:T(8,128)S(1)}, u32[]{:S(2)}, u32[]{:S(2)}) collective-permute-start(f32[512,128]{1,0:T(8,128)S(1)} %shard_map.62), channel_id=1, source_target_pairs={{0,6},{1,7},{2,0},{3,1},{4,2},{5,3},{6,4},{7,5},{8,14},{9,15},{10,... | collective-permute-start | bytes 786440 | tf_op jit(solution)/shard_map/ppermute | solution.py:324
  92.1 20.6 %collective-permute-start.19 = (f32[512,128]{1,0:T(8,128)S(1)}, f32[512,128]{1,0:T(8,128)S(1)}, u32[]{:S(2)}, u32[]{:S(2)}) collective-permute-start(f32[512,128]{1,0:T(8,128)S(1)} %shard_map.63), channel_id=1, source_target_pairs={{0,4},{1,5},{2,6},{3,7},{4,0},{5,1},{6,2},{7,3},{8,12},{9,13},{10,... | collective-permute-start | bytes 786440 | tf_op jit(solution)/shard_map/ppermute | solution.py:324
  95.5 20.8 %collective-permute-start.20 = (f32[512,128]{1,0:T(8,128)S(1)}, f32[512,128]{1,0:T(8,128)S(1)}, u32[]{:S(2)}, u32[]{:S(2)}) collective-permute-start(f32[512,128]{1,0:T(8,128)S(1)} %shard_map.64), channel_id=1, source_target_pairs={{0,2},{1,3},{2,4},{3,5},{4,6},{5,7},{6,0},{7,1},{8,10},{9,11},{10,... | collective-permute-start | bytes 786440 | tf_op jit(solution)/shard_map/ppermute | solution.py:324
where the time goes:
time: 118 us
  waiting for transfers between devices  54.3 us (46%)
  Pallas kernels  38.5 us (33%)
  starting transfers between devices  21.1 us (18%)
  other arithmetic  2.04 us (2%)
  local copies, waits for them, and re-layouts  1.92 us (2%)
    ppermute x21, waiting for transfers between devices, send(): return lax.ppermute(x, axis, pairs)  54.3 us
    pallas_call x11, Pallas kernels, call(): pl.pallas_call(kernel, out_shape=out_shape, in_specs=specs, out_specs=out...  38.5 us
    ppermute x21, starting transfers between devices, send(): return lax.ppermute(x, axis, pairs)  21.1 us
  transfers between devices with their start and end apart: 21, of which 14 were waited for; matrix products, arithmetic and copies ran while one was open for 0% of the time, Pallas kernels for 16%

commit v1 on v0

--- a/solution.py
+++ b/solution.py
@@ -148,74 +148,64 @@
             vsec_ref[at] = vs[r][d]
 
 
-def near_kernel(heads, ring, length, width, scal, *refs):
-    qs = refs[:heads]
-    wk_ref, yz_ref, kmcat_ref, vb_ref = refs[heads : heads + 4]
-    qcat_ref, ml_ref, acc_ref = refs[heads + 4 : heads + 7]
-    q_s, s_s = refs[heads + 7 :]
+def near_kernel(d, heads, ring, length, width, scal, q_ref, *refs):
+    wk_ref, yz_ref, kmcat_ref, vb_ref, qcat_ref, ml_ref, acc_ref, q_s, s_s = refs
     place, low = scal[0], scal[1]
-    rows = qs[0].shape[0]
+    rows = q_ref.shape[0]
     scale = width ** (-0.5) * LOG2_E
     blocks = heads * ring
     keys = blocks * length
     token = lax.rem(lax.broadcasted_iota(jnp.int32, (rows, length), 0), length)
     causal = token >= lax.broadcasted_iota(jnp.int32, (rows, length), 1)
     lane_id = lax.broadcasted_iota(jnp.int32, (rows // 2, 128), 1)
-    for d in range(heads):
-        q_s[d] = qs[d][...]
 
     def at(b):
         return pl.ds(pl.multiple_of(b * length, length), length)
 
-    def piece(d, carry):
-        t = lax.rem(place - d + heads, heads)
-        b_own = t * ring + low
-        qf = q_s[d]
-        q = qf.astype(BF16)
-        both = mm(jnp.concatenate([q, q], axis=1), wk_ref[t])
-        qw = jnp.where(causal, both[:, :length], 0.0)
-        u = mm(left_cat(qw), yz_ref[t])
-        q_s[d] = (qf - u[:, length:]) * scale
-        s_s[:, at(b_own)] = jnp.where(causal, (both[:, length:] - u[:, :length]) * scale, LOW)
-
-        def clear(b, c):
-            s_s[:, at(b)] = jnp.full((rows, length), LOW, F32)
-            return c
-
-        lax.fori_loop(b_own + 1, blocks, clear, 0)
-
-        def step(i, c):
-            b = b_own - 1 - i
-            both = mm(left_cat(q_s[d]), kmcat_ref[b])
-            s_s[:, at(b)] = both[:, :length]
-            q_s[d] = both[:, length:]
-            return c
-
-        lax.fori_loop(0, b_own, step, 0)
-        qcat_ref[d] = left_cat(q_s[d])
-
-        def finish(n):
-            for half in range(2):
-                part = slice(half * rows // 2, (half + 1) * rows // 2)
-                s = s_s[part, :n]
-                top = jnp.max(s, -1, keepdims=True)
-                p = jnp.exp2(s - top)
-                ml_ref[d, part] = jnp.where(lane_id < 64, top, jnp.sum(p, -1, keepdims=True))
-                acc_ref[d, part] = mm(p.astype(BF16), vb_ref[:n])
-
-        small = b_own < blocks // 2
-
-        @pl.when(small)
-        def _():
-            finish(keys // 2)
-
-        @pl.when(jnp.logical_not(small))
-        def _():
-            finish(keys)
-
-        return carry
-
-    lax.fori_loop(0, heads, piece, 0)
+    t = lax.rem(place - d + heads, heads)
+    b_own = t * ring + low
+    qf = q_ref[...]
+    q = qf.astype(BF16)
+    both = mm(jnp.concatenate([q, q], axis=1), wk_ref[t])
+    qw = jnp.where(causal, both[:, :length], 0.0)
+    u = mm(left_cat(qw), yz_ref[t])
+    q_s[...] = (qf - u[:, length:]) * scale
+    s_s[:, at(b_own)] = jnp.where(causal, (both[:, length:] - u[:, :length]) * scale, LOW)
+
+    def clear(b, c):
+        s_s[:, at(b)] = jnp.full((rows, length), LOW, F32)
+        return c
+
+    lax.fori_loop(b_own + 1, blocks, clear, 0)
+
+    def step(i, c):
+        b = b_own - 1 - i
+        both = mm(left_cat(q_s[...]), kmcat_ref[b])
+        s_s[:, at(b)] = both[:, :length]
+        q_s[...] = both[:, length:]
+        return c
+
+    lax.fori_loop(0, b_own, step, 0)
+    qcat_ref[...] = left_cat(q_s[...])
+
+    def finish(n):
+        for half in range(2):
+            part = slice(half * rows // 2, (half + 1) * rows // 2)
+            s = s_s[part, :n]
+            top = jnp.max(s, -1, keepdims=True)
+            p = jnp.exp2(s - top)
+            ml_ref[part] = jnp.where(lane_id < 64, top, jnp.sum(p, -1, keepdims=True))
+            acc_ref[part] = mm(p.astype(BF16), vb_ref[:n])
+
+    small = b_own < blocks // 2
+
+    @pl.when(small)
+    def _():
+        finish(keys // 2)
+
+    @pl.when(jnp.logical_not(small))
+    def _():
+        finish(keys)
 
 
 def prep_kernel(hops, scal, *refs):
@@ -258,27 +248,18 @@
         got_map = moved[:, keys:]
 
 
-def far_kernel(first, parts, scal, q_ref, ml_ref, acc_ref, k_ref, v_ref, *refs):
-    count = len(refs) - 3
-    outs = refs[:count]
-    m_s, l_s, a_s = refs[count:]
-    rows = q_ref.shape[1]
-    size = rows // parts
-    spots = [(d, p) for d in range(count) for p in range(parts)]
-    for i, (d, p) in enumerate(spots):
-        part = slice(p * size, (p + 1) * size)
-        m_s[i] = ml_ref[first + d, part, 0:1]
-        l_s[i] = ml_ref[first + d, part, 64:65]
-        a_s[i] = acc_ref[first + d, part]
-
-    def scores(i, sec):
-        d, p = spots[i]
-        return mm(q_ref[first + d, p * size : (p + 1) * size], k_ref[sec])
+def far_kernel(parts, scal, q_ref, ml_ref, acc_ref, k_ref, v_ref, out_ref, m_s, l_s, a_s):
+    size = q_ref.shape[0] // parts
+    spots = [slice(p * size, (p + 1) * size) for p in range(parts)]
+    for i, part in enumerate(spots):
+        m_s[i] = ml_ref[part, 0:1]
+        l_s[i] = ml_ref[part, 64:65]
+        a_s[i] = acc_ref[part]
 
     def step(sec, c):
-        s = scores(0, sec)
-        for i in range(len(spots)):
-            coming = scores(i + 1, sec) if i + 1 < len(spots) else None
+        s = mm(q_ref[spots[0]], k_ref[sec])
+        for i in range(parts):
+            coming = mm(q_ref[spots[i + 1]], k_ref[sec]) if i + 1 < parts else None
             old = m_s[i]
             top = jnp.maximum(old, jnp.max(s, -1, keepdims=True))
             p = jnp.exp2(s - top)
@@ -290,8 +271,8 @@
         return c
 
     lax.fori_loop(0, jnp.minimum(scal[2], k_ref.shape[0]), step, 0)
-    for i, (d, p) in enumerate(spots):
-        outs[d][p * size : (p + 1) * size] = a_s[i] / l_s[i]
+    for i, part in enumerate(spots):
+        out_ref[part] = a_s[i] / l_s[i]
 
 
 def join_kernel(heads, scal, *refs):
@@ -320,9 +301,6 @@
     def across(d):
         return [(k, (k // ring) * ring + (k % ring + d) % ring) for k in range(key_count)]
 
-    def send(x, axis, pairs):
-        return lax.ppermute(x, axis, pairs)
-
     def chunks(x):
         return [
             lax.dynamic_index_in_dim(x, lax.rem(place + d, heads), 0, keepdims=False)
@@ -330,10 +308,12 @@
         ]
 
     def deal(own):
-        return [own[0]] + [send(own[d], "key", around(d)) for d in range(1, heads)]
+        return [own[0]] + [
+            lax.ppermute(own[d], "key", around(d)) for d in range(1, heads)
+        ]
 
     def gather(x):
-        return [x] + [send(x, "key", across(d)) for d in range(1, ring)]
+        return [x] + [lax.ppermute(x, "key", across(d)) for d in range(1, ring)]
 
     def by_head(x):
         return jnp.transpose(x.astype(F32), (1, 0, 2))
@@ -387,28 +367,29 @@
 
     pair = [(s, s ^ 1) for s in range(sec_count)]
     rise = [(s, s + 1) for s in range(0, sec_count, 2)]
-    v_far = [send(vsec, "sec", rise)]
-    k_far = [send(packet, "sec", rise)]
+    v_far = [lax.ppermute(vsec, "sec", rise)]
+    k_far = [lax.ppermute(packet, "sec", rise)]
     for p in range(1, hops + 1):
         line = [(s, s + 2 * p) for s in range(sec_count - 2 * p)]
-        v_got = arrange(gather(send(v_own, "sec", line)))[1]
-        k_got = send(packet, "sec", line)
-        v_far += [v_got, send(v_got, "sec", pair)]
-        k_far += [k_got, send(k_got, "sec", pair)]
-    qcat, ml, acc = call(
-        functools.partial(near_kernel, heads, ring, length, width),
-        (
-            sds((heads, rows, 3 * width), BF16),
-            sds((heads, rows, 128), F32),
-            sds((heads, rows, width), F32),
-        ),
-        qs + [wk, yz, kmcat, vb],
-        scratch=[pltpu.VMEM((heads, rows, width), F32), pltpu.VMEM((rows, keys), F32)],
-        scalars=scal,
-        flops=heads * blocks // 2 * rows * width * length * 14,
-        nbytes=heads * rows * width * 16,
-        exps=heads * blocks // 2 * rows * length,
-    )
+        v_got = arrange(gather(lax.ppermute(v_own, "sec", line)))[1]
+        k_got = lax.ppermute(packet, "sec", line)
+        v_far += [v_got, lax.ppermute(v_got, "sec", pair)]
+        k_far += [k_got, lax.ppermute(k_got, "sec", pair)]
+
+    def near(d):
+        return call(
+            functools.partial(near_kernel, d, heads, ring, length, width),
+            (sds((rows, 3 * width), BF16), sds((rows, 128), F32), sds((rows, width), F32)),
+            [qs[d], wk, yz, kmcat, vb],
+            scratch=[pltpu.VMEM((rows, width), F32), pltpu.VMEM((rows, keys), F32)],
+            scalars=scal,
+            flops=blocks // 2 * rows * width * length * 14,
+            nbytes=rows * width * 16,
+            exps=blocks // 2 * rows * length,
+        )
+
+    order = [heads // 2] + [d for d in range(1, heads) if d != heads // 2] + [0]
+    found = {d: near(d) for d in [0] + order[:-1]}
     far_count = 2 * hops + 1
     kc, vc = call(
         functools.partial(prep_kernel, hops),
@@ -421,27 +402,26 @@
     )
     parts = 2
 
-    def far(first, count):
-        got = call(
-            functools.partial(far_kernel, first, parts),
-            (sds((rows, width), F32),) * count,
-            [qcat, ml, acc, kc, vc],
+    def far(d):
+        return call(
+            functools.partial(far_kernel, parts),
+            sds((rows, width), F32),
+            list(found[d]) + [kc, vc],
             scratch=[
-                pltpu.VMEM((count * parts, rows // parts, 1), F32),
-                pltpu.VMEM((count * parts, rows // parts, 1), F32),
-                pltpu.VMEM((count * parts, rows // parts, width), F32),
+                pltpu.VMEM((parts, rows // parts, 1), F32),
+                pltpu.VMEM((parts, rows // parts, 1), F32),
+                pltpu.VMEM((parts, rows // parts, width), F32),
             ],
             scalars=scal,
-            flops=count * rows * far_count * keys * width * 8,
-            nbytes=count * rows * width * 20 + far_count * keys * width * 8,
-            exps=count * rows * far_count * keys,
+            flops=rows * far_count * keys * width * 8,
+            nbytes=rows * width * 20 + far_count * keys * width * 8,
+            exps=rows * far_count * keys,
         )
-        return list(got)
 
     back = [None] * heads
-    for d in [heads // 2] + [d for d in range(1, heads) if d != heads // 2] + [0]:
-        (piece,) = far(d, 1)
-        back[d] = send(piece, "key", around(-d)) if d else piece
+    for d in order:
+        piece = far(d)
+        back[d] = lax.ppermute(piece, "key", around(-d)) if d else piece
     joined = call(
         functools.partial(join_kernel, heads),
         sds((heads, rows, width), BF16),

time: 118 us -> 116 us (0.983)
  the two profiles are of different devices: /device:TPU:23 before, /device:TPU:11 now
where the time goes in v1:
time: 116 us
  waiting for transfers between devices  43.4 us (37%)
  Pallas kernels  39 us (34%)
  starting transfers between devices  29.6 us (26%)
  other arithmetic  2.04 us (2%)
  local copies, waits for them, and re-layouts  1.92 us (2%)
    pallas_call x14, Pallas kernels, call(): pl.pallas_call(kernel, out_shape=out_shape, in_specs=specs, out_specs=out...  39 us
    ppermute x9, waiting for transfers between devices, deal(): lax.ppermute(own[d], 'key', around(d))  23 us
    ppermute x9, starting transfers between devices, deal(): lax.ppermute(own[d], 'key', around(d))  11.2 us
    ppermute x1, waiting for transfers between devices, steps(): k_got = lax.ppermute(packet, 'sec', line)  9.93 us
    ppermute x3, waiting for transfers between devices, steps(): back[d] = lax.ppermute(piece, 'key', around(-d)) if d else piece  7.91 us
    ppermute x3, starting transfers between devices, steps(): back[d] = lax.ppermute(piece, 'key', around(-d)) if d else piece  7.04 us
    ppermute x3, starting transfers between devices, gather(): return [x] + [lax.ppermute(x, 'key', across(d)) for d in range(1, ring)]  2.84 us
    ppermute x3, waiting for transfers between devices, gather(): return [x] + [lax.ppermute(x, 'key', across(d)) for d in range(1, ring)]  2.53 us
  transfers between devices with their start and end apart: 21, of which 12 were waited for; matrix products, arithmetic and copies ran while one was open for 0% of the time, Pallas kernels for 24%

profile of v1, /device:TPU:11, one launch (start us, length us, event | category | flops | bytes accessed | tf_op | source)
XLA Modules:
  0.0 116.2 jit_solution(1719760843552896273)
XLA Ops:
  2.3 2.4 %collective-permute-start.1 = (f32[264,128]{1,0:T(8,128)S(1)}, f32[264,128]{1,0:T(8,128)S(1)}, u32[]{:S(2)}, u32[]{:S(2)}) collective-permute-start(f32[264,128]{1,0:T(8,128)S(1)} %bitcast.42), channel_id=1, source_target_pairs={{0,4},{1,5},{2,6},{3,7},{4,0},{5,1},{6,2},{7,3},{8,12},{9,13},{10,... | collective-permute-start | bytes 405512 | tf_op jit(solution)/shard_map/ppermute | solution.py:312
  6.2 7.5 %collective-permute-done.1.refs_2_ = f32[264,128]{1,0:T(8,128)S(1)} collective-permute-done((f32[264,128]{1,0:T(8,128)S(1)}, f32[264,128]{1,0:T(8,128)S(1)}, u32[]{:S(2)}, u32[]{:S(2)}) %collective-permute-start.1) | collective-permute-done | bytes 135200 | tf_op jit(solution)/shard_map/ppermute | solution.py:312
  13.7 1.7 %collective-permute-done.2.refs_3_ = f32[264,128]{1,0:T(8,128)S(1)} collective-permute-done((f32[264,128]{1,0:T(8,128)S(1)}, f32[264,128]{1,0:T(8,128)S(1)}, u32[]{:S(2)}, u32[]{:S(2)}) %collective-permute-start.2) | collective-permute-done | bytes 135200 | tf_op jit(solution)/shard_map/ppermute | solution.py:312
  16.6 4.3 %shard_map.55 = (f32[4,128,256]{2,1,0:T(8,128)S(1)}, bf16[4,256,256]{2,1,0:T(8,128)(2,1)S(1)}, bf16[4,384,256]{2,1,0:T(8,128)(2,1)S(1)}) custom-call(s32[3]{0:T(128)S(1)} %pad_add_fusion.scal, f32[264,128]{1,0:T(8,128)S(1)} %bitcast.37, f32[264,128]{1,0:T(8,128)S(1)} %collective-permute-done.refs_1_, f32[264,128]{1,0:T(8,128)S(1)} %collective-permute-done.1.refs_2_, ...), custom_call_target="tpu_custom_call" | custom-call | flops 1006632960 | bytes 2621440 | tf_op jit(solution)/shard_map/pallas_call | solution.py:49
  22.6 3.4 %collective-permute-start.5 = (f32[128,128]{1,0:T(8,128)S(1)}, f32[128,128]{1,0:T(8,128)S(1)}, u32[]{:S(2)}, u32[]{:S(2)}) collective-permute-start(f32[128,128]{1,0:T(8,128)S(1)} %bitcast.45), channel_id=1, source_target_pairs={{0,4},{1,5},{2,6},{3,7},{4,0},{5,1},{6,2},{7,3},{8,12},{9,13},{10,... | collective-permute-start | bytes 196616 | tf_op jit(solution)/shard_map/ppermute | solution.py:312
  26.7 1.8 %collective-permute-done.5 = f32[128,128]{1,0:T(8,128)S(1)} collective-permute-done((f32[128,128]{1,0:T(8,128)S(1)}, f32[128,128]{1,0:T(8,128)S(1)}, u32[]{:S(2)}, u32[]{:S(2)}) %collective-permute-start.5) | collective-permute-done | bytes 65568 | tf_op jit(solution)/shard_map/ppermute | solution.py:312
  28.5 1.7 %collective-permute-done.4 = f32[128,128]{1,0:T(8,128)S(1)} collective-permute-done((f32[128,128]{1,0:T(8,128)S(1)}, f32[128,128]{1,0:T(8,128)S(1)}, u32[]{:S(2)}, u32[]{:S(2)}) %collective-permute-start.4) | collective-permute-done | bytes 65568 | tf_op jit(solution)/shard_map/ppermute | solution.py:312
  31.5 2.5 %collective-permute-done.3.refs_1_ = f32[4,128,256]{2,1,0:T(8,128)S(1)} collective-permute-done((f32[4,128,256]{2,1,0:T(8,128)S(1)}, f32[4,128,256]{2,1,0:T(8,128)S(1)}, u32[]{:S(2)}, u32[]{:S(2)}) %collective-permute-start.3) | collective-permute-done | bytes 524320 | tf_op jit(solution)/shard_map/ppermute | solution.py:316
  34.0 2.1 %shard_map.56 = (bf16[8,384,256]{2,1,0:T(8,128)(2,1)S(1)}, f32[128,1152]{1,0:T(8,128)S(1)}) custom-call(s32[3]{0:T(128)S(1)} %pad_add_fusion.scal, f32[4,128,256]{2,1,0:T(8,128)S(1)} %get-tuple-element.29.refs_0_, f32[4,128,256]{2,1,0:T(8,128)S(1)} %collective-permute-done.3.refs_1_), custom_call_target="tpu_custom_call" | custom-call | flops 201326592 | bytes 4194304 | tf_op jit(solution)/shard_map/pallas_call | solution.py:49
  41.6 9.9 %collective-permute-done.9.refs_1_ = f32[128,1152]{1,0:T(8,128)S(1)} collective-permute-done((f32[128,1152]{1,0:T(8,128)S(1)}, f32[128,1152]{1,0:T(8,128)S(1)}, u32[]{:S(2)}, u32[]{:S(2)}) %collective-permute-start.9) | collective-permute-done | bytes 589856 | tf_op jit(solution)/shard_map/ppermute | solution.py:375
  51.5 2.2 %collective-permute-start.10 = (f32[128,1152]{1,0:T(8,128)S(1)}, f32[128,1152]{1,0:T(8,128)S(1)}, u32[]{:S(2)}, u32[]{:S(2)}) collective-permute-start(f32[128,1152]{1,0:T(8,128)S(1)} %collective-permute-done.9.refs_1_), channel_id=1, source_target_pairs={{0,8},{8,0},{16,24},{24,16},{1,9},{9,1},{17,25},{25,17},{2,10},{10... | collective-permute-start | bytes 1769480 | tf_op jit(solution)/shard_map/ppermute | solution.py:377
  59.5 6.9 %collective-permute-done.17.q_ref = f32[512,128]{1,0:T(8,128)S(1)} collective-permute-done((f32[512,128]{1,0:T(8,128)S(1)}, f32[512,128]{1,0:T(8,128)S(1)}, u32[]{:S(2)}, u32[]{:S(2)}) %collective-permute-start.17) | collective-permute-done | bytes 262176 | tf_op jit(solution)/shard_map/ppermute | solution.py:312
  67.8 3.0 %shard_map.66 = (bf16[512,384]{1,0:T(8,128)(2,1)S(1)}, f32[512,128]{1,0:T(8,128)S(1)}, f32[512,128]{1,0:T(8,128)S(1)}) custom-call(s32[3]{0:T(128)S(1)} %pad_add_fusion.scal, f32[512,128]{1,0:T(8,128)S(1)} %collective-permute-done.19.q_ref, bf16[4,256,256]{2,1,0:T(8,128)(2,1)S(1)} %get-tuple-element.27.refs_0_, ...), custom_call_target="tpu_custom_call" | custom-call | flops 469762048 | bytes 1048576 | tf_op jit(solution)/shard_map/pallas_call | solution.py:49
  70.9 3.6 %shard_map.64 = (bf16[512,384]{1,0:T(8,128)(2,1)S(1)}, f32[512,128]{1,0:T(8,128)S(1)}, f32[512,128]{1,0:T(8,128)S(1)}) custom-call(s32[3]{0:T(128)S(1)} %pad_add_fusion.scal, f32[512,128]{1,0:T(8,128)S(1)} %collective-permute-done.17.q_ref, bf16[4,256,256]{2,1,0:T(8,128)(2,1)S(1)} %get-tuple-element.27.refs_0_, ...), custom_call_target="tpu_custom_call" | custom-call | flops 469762048 | bytes 1048576 | tf_op jit(solution)/shard_map/pallas_call | solution.py:49
  76.0 1.8 %shard_map.62 = (bf16[512,384]{1,0:T(8,128)(2,1)S(1)}, f32[512,128]{1,0:T(8,128)S(1)}, f32[512,128]{1,0:T(8,128)S(1)}) custom-call(s32[3]{0:T(128)S(1)} %pad_add_fusion.scal, f32[512,128]{1,0:T(8,128)S(1)} %collective-permute-done.15.q_ref, bf16[4,256,256]{2,1,0:T(8,128)(2,1)S(1)} %get-tuple-element.27.refs_0_, ...), custom_call_target="tpu_custom_call" | custom-call | flops 469762048 | bytes 1048576 | tf_op jit(solution)/shard_map/pallas_call | solution.py:49
  77.8 1.6 %shard_map.60 = (bf16[3,384,1024]{2,1,0:T(8,128)(2,1)S(1)}, bf16[3,1024,128]{2,1,0:T(8,128)(2,1)S(1)}) custom-call(s32[3]{0:T(128)S(1)} %pad_add_fusion.scal, f32[128,1152]{1,0:T(8,128)S(1)} %collective-permute-done.8.refs_0_, f32[128,1152]{1,0:T(8,128)S(1)} %collective-permute-done.9.refs_1_, f32[128,1152]{1,0:T(8,128)S(1)} %collective-permute-done.10.refs_2_, ...), custom_call_target="tpu_custom_call" | custom-call | flops 301989888 | bytes 6291456 | tf_op jit(solution)/shard_map/pallas_call | solution.py:49
  79.4 4.4 %shard_map.67 = f32[512,128]{1,0:T(8,128)S(1)} custom-call(s32[3]{0:T(128)S(1)} %pad_add_fusion.scal, bf16[512,384]{1,0:T(8,128)(2,1)S(1)} %get-tuple-element.46.q_ref, f32[512,128]{1,0:T(8,128)S(1)} %get-tuple-element.47.ml_ref, f32[512,128]{1,0:T(8,128)S(1)} %get-tuple-element.48.acc_ref, bf16[3,384,1024]{2,1,0:T(8,128)(2,1)S(1)} %get-tuple-element.38.k_ref, ...), custom_call_target="tpu_custom_call" | custom-call | flops 1610612736 | bytes 4456448 | tf_op jit(solution)/shard_map/pallas_call | solution.py:49
  83.9 4.5 %shard_map.65 = f32[512,128]{1,0:T(8,128)S(1)} custom-call(s32[3]{0:T(128)S(1)} %pad_add_fusion.scal, bf16[512,384]{1,0:T(8,128)(2,1)S(1)} %get-tuple-element.43.q_ref, f32[512,128]{1,0:T(8,128)S(1)} %get-tuple-element.44.ml_ref, f32[512,128]{1,0:T(8,128)S(1)} %get-tuple-element.45.acc_ref, bf16[3,384,1024]{2,1,0:T(8,128)(2,1)S(1)} %get-tuple-element.38.k_ref, ...), custom_call_target="tpu_custom_call" | custom-call | flops 1610612736 | bytes 4456448 | tf_op jit(solution)/shard_map/pallas_call | solution.py:49
  88.4 6.9 %collective-permute-start.18 = (f32[512,128]{1,0:T(8,128)S(1)}, f32[512,128]{1,0:T(8,128)S(1)}, u32[]{:S(2)}, u32[]{:S(2)}) collective-permute-start(f32[512,128]{1,0:T(8,128)S(1)} %shard_map.65), channel_id=1, source_target_pairs={{0,4},{1,5},{2,6},{3,7},{4,0},{5,1},{6,2},{7,3},{8,12},{9,13},{10,... | collective-permute-start | bytes 786440 | tf_op jit(solution)/shard_map/ppermute | solution.py:424
  95.3 4.4 %shard_map.63 = f32[512,128]{1,0:T(8,128)S(1)} custom-call(s32[3]{0:T(128)S(1)} %pad_add_fusion.scal, bf16[512,384]{1,0:T(8,128)(2,1)S(1)} %get-tuple-element.40.q_ref, f32[512,128]{1,0:T(8,128)S(1)} %get-tuple-element.41.ml_ref, f32[512,128]{1,0:T(8,128)S(1)} %get-tuple-element.42.acc_ref, bf16[3,384,1024]{2,1,0:T(8,128)(2,1)S(1)} %get-tuple-element.38.k_ref, ...), custom_call_target="tpu_custom_call" | custom-call | flops 1610612736 | bytes 4456448 | tf_op jit(solution)/shard_map/pallas_call | solution.py:49
  99.8 2.3 %shard_map.58 = (bf16[512,384]{1,0:T(8,128)(2,1)S(1)}, f32[512,128]{1,0:T(8,128)S(1)}, f32[512,128]{1,0:T(8,128)S(1)}) custom-call(s32[3]{0:T(128)S(1)} %pad_add_fusion.scal, f32[512,128]{1,0:T(8,128)S(1)} %get-tuple-element.52.q_ref, bf16[4,256,256]{2,1,0:T(8,128)(2,1)S(1)} %get-tuple-element.27.refs_0_, ...), custom_call_target="tpu_custom_call" | custom-call | flops 469762048 | bytes 1048576 | tf_op jit(solution)/shard_map/pallas_call | solution.py:49
  102.1 4.4 %shard_map.61.refs_0_ = f32[512,128]{1,0:T(8,128)S(1)} custom-call(s32[3]{0:T(128)S(1)} %pad_add_fusion.scal, bf16[512,384]{1,0:T(8,128)(2,1)S(1)} %get-tuple-element.32.q_ref, f32[512,128]{1,0:T(8,128)S(1)} %get-tuple-element.33.ml_ref, f32[512,128]{1,0:T(8,128)S(1)} %get-tuple-element.34.acc_ref, bf16[3,384,1024]{2,1,0:T(8,128)(2,1)S(1)} %get-tuple-element.38.k_ref, ...), custom_call_target="tpu_custom_call" | custom-call | flops 1610612736 | bytes 4456448 | tf_op jit(solution)/shard_map/pallas_call | solution.py:49
  106.5 4.9 %collective-permute-done.18.refs_2_ = f32[512,128]{1,0:T(8,128)S(1)} collective-permute-done((f32[512,128]{1,0:T(8,128)S(1)}, f32[512,128]{1,0:T(8,128)S(1)}, u32[]{:S(2)}, u32[]{:S(2)}) %collective-permute-start.18) | collective-permute-done | bytes 262176 | tf_op jit(solution)/shard_map/ppermute | solution.py:424
  111.4 3.0 %collective-permute-done.16.refs_1_ = f32[512,128]{1,0:T(8,128)S(1)} collective-permute-done((f32[512,128]{1,0:T(8,128)S(1)}, f32[512,128]{1,0:T(8,128)S(1)}, u32[]{:S(2)}, u32[]{:S(2)}) %collective-permute-start.16) | collective-permute-done | bytes 262176 | tf_op jit(solution)/shard_map/ppermute | solution.py:424
  (46 shorter events, 24.7 us)
Async XLA Ops:
  1.8 20.4 %copy-start.1 = (bf16[128,4,128]{2,1,0:T(4,128)(2,1)S(1)}, bf16[128,4,128]{2,1,0:T(4,128)(2,1)}, u32[]{:S(2)}) copy-start(bf16[128,4,128]{2,1,0:T(4,128)(2,1)} %param.7) | copy-start | bytes 393220
  2.3 11.4 %collective-permute-start.1 = (f32[264,128]{1,0:T(8,128)S(1)}, f32[264,128]{1,0:T(8,128)S(1)}, u32[]{:S(2)}, u32[]{:S(2)}) collective-permute-start(f32[264,128]{1,0:T(8,128)S(1)} %bitcast.42), channel_id=1, source_target_pairs={{0,4},{1,5},{2,6},{3,7},{4,0},{5,1},{6,2},{7,3},{8,12},{9,13},{10,... | collective-permute-start | bytes 405512 | tf_op jit(solution)/shard_map/ppermute | solution.py:312
  4.7 10.8 %collective-permute-start.2 = (f32[264,128]{1,0:T(8,128)S(1)}, f32[264,128]{1,0:T(8,128)S(1)}, u32[]{:S(2)}, u32[]{:S(2)}) collective-permute-start(f32[264,128]{1,0:T(8,128)S(1)} %bitcast.41), channel_id=1, source_target_pairs={{0,6},{1,7},{2,0},{3,1},{4,2},{5,3},{6,4},{7,5},{8,14},{9,15},{10,... | collective-permute-start | bytes 405512 | tf_op jit(solution)/shard_map/ppermute | solution.py:312
  4.8 11.8 %collective-permute-start = (f32[264,128]{1,0:T(8,128)S(1)}, f32[264,128]{1,0:T(8,128)S(1)}, u32[]{:S(2)}, u32[]{:S(2)}) collective-permute-start(f32[264,128]{1,0:T(8,128)S(1)} %bitcast.40), channel_id=1, source_target_pairs={{0,2},{1,3},{2,4},{3,5},{4,6},{5,7},{6,0},{7,1},{8,10},{9,11},{10,... | collective-permute-start | bytes 405512 | tf_op jit(solution)/shard_map/ppermute | solution.py:312
  16.6 20.8 %copy-start = (bf16[128,16,128]{2,1,0:T(8,128)(2,1)S(1)}, bf16[128,16,128]{2,1,0:T(8,128)(2,1)}, u32[]{:S(2)}) copy-start(bf16[128,16,128]{2,1,0:T(8,128)(2,1)} %param.5) | copy-start | bytes 1572868
  20.9 13.1 %collective-permute-start.3 = (f32[4,128,256]{2,1,0:T(8,128)S(1)}, f32[4,128,256]{2,1,0:T(8,128)S(1)}, u32[]{:S(2)}, u32[]{:S(2)}) collective-permute-start(f32[4,128,256]{2,1,0:T(8,128)S(1)} %get-tuple-element.29.refs_0_), channel_id=1, source_target_pairs={{0,1},{1,0},{2,3},{3,2},{4,5},{5,4},{6,7},{7,6},{8,9},{9,8},{10,11... | collective-permute-start | bytes 1572872 | tf_op jit(solution)/shard_map/ppermute | solution.py:316
  22.5 4.2 %collective-permute-start.6 = (f32[128,128]{1,0:T(8,128)S(1)}, f32[128,128]{1,0:T(8,128)S(1)}, u32[]{:S(2)}, u32[]{:S(2)}) collective-permute-start(f32[128,128]{1,0:T(8,128)S(1)} %bitcast.47), channel_id=1, source_target_pairs={{0,6},{1,7},{2,0},{3,1},{4,2},{5,3},{6,4},{7,5},{8,14},{9,15},{10,... | collective-permute-start | bytes 196616 | tf_op jit(solution)/shard_map/ppermute | solution.py:312
  22.6 5.9 %collective-permute-start.5 = (f32[128,128]{1,0:T(8,128)S(1)}, f32[128,128]{1,0:T(8,128)S(1)}, u32[]{:S(2)}, u32[]{:S(2)}) collective-permute-start(f32[128,128]{1,0:T(8,128)S(1)} %bitcast.45), channel_id=1, source_target_pairs={{0,4},{1,5},{2,6},{3,7},{4,0},{5,1},{6,2},{7,3},{8,12},{9,13},{10,... | collective-permute-start | bytes 196616 | tf_op jit(solution)/shard_map/ppermute | solution.py:312
  26.0 4.2 %collective-permute-start.4 = (f32[128,128]{1,0:T(8,128)S(1)}, f32[128,128]{1,0:T(8,128)S(1)}, u32[]{:S(2)}, u32[]{:S(2)}) collective-permute-start(f32[128,128]{1,0:T(8,128)S(1)} %bitcast.43), channel_id=1, source_target_pairs={{0,2},{1,3},{2,4},{3,5},{4,6},{5,7},{6,0},{7,1},{8,10},{9,11},{10,... | collective-permute-start | bytes 196616 | tf_op jit(solution)/shard_map/ppermute | solution.py:312
  30.2 8.6 %collective-permute-start.12 = (f32[4,128,128]{2,1,0:T(8,128)S(1)}, f32[4,128,128]{2,1,0:T(8,128)S(1)}, u32[]{:S(2)}, u32[]{:S(2)}) collective-permute-start(f32[4,128,128]{2,1,0:T(8,128)S(1)} %pad_maximum_fusion.refs_0_), channel_id=1, source_target_pairs={{0,16},{8,24},{1,17},{9,25},{2,18},{10,26},{3,19},{11,27},{4,20},{... | collective-permute-start | bytes 786440 | tf_op jit(solution)/shard_map/ppermute | solution.py:374
  36.1 15.4 %collective-permute-start.9 = (f32[128,1152]{1,0:T(8,128)S(1)}, f32[128,1152]{1,0:T(8,128)S(1)}, u32[]{:S(2)}, u32[]{:S(2)}) collective-permute-start(f32[128,1152]{1,0:T(8,128)S(1)} %get-tuple-element.35), channel_id=1, source_target_pairs={{0,16},{8,24},{1,17},{9,25},{2,18},{10,26},{3,19},{11,27},{4,20},{... | collective-permute-start | bytes 1769480 | tf_op jit(solution)/shard_map/ppermute | solution.py:375
  37.5 16.2 %collective-permute-start.7 = (f32[4,128,128]{2,1,0:T(8,128)S(1)}, f32[4,128,128]{2,1,0:T(8,128)S(1)}, u32[]{:S(2)}, u32[]{:S(2)}) collective-permute-start(f32[4,128,128]{2,1,0:T(8,128)S(1)} %pad_maximum_fusion.refs_0_), channel_id=1, source_target_pairs={{0,1},{1,0},{2,3},{3,2},{4,5},{5,4},{6,7},{7,6},{8,9},{9,8},{10,11... | collective-permute-start | bytes 786440 | tf_op jit(solution)/shard_map/ppermute | solution.py:316
  38.8 16.9 %collective-permute-start.13 = (f32[4,128,128]{2,1,0:T(8,128)S(1)}, f32[4,128,128]{2,1,0:T(8,128)S(1)}, u32[]{:S(2)}, u32[]{:S(2)}) collective-permute-start(f32[4,128,128]{2,1,0:T(8,128)S(1)} %collective-permute-done.12.refs_0_), channel_id=1, source_target_pairs={{0,1},{1,0},{2,3},{3,2},{4,5},{5,4},{6,7},{7,6},{8,9},{9,8},{10,11... | collective-permute-start | bytes 786440 | tf_op jit(solution)/shard_map/ppermute | solution.py:316
  39.1 19.2 %collective-permute-start.19 = (f32[512,128]{1,0:T(8,128)S(1)}, f32[512,128]{1,0:T(8,128)S(1)}, u32[]{:S(2)}, u32[]{:S(2)}) collective-permute-start(f32[512,128]{1,0:T(8,128)S(1)} %get-tuple-element.49), channel_id=1, source_target_pairs={{0,6},{1,7},{2,0},{3,1},{4,2},{5,3},{6,4},{7,5},{8,14},{9,15},{10,... | collective-permute-start | bytes 786440 | tf_op jit(solution)/shard_map/ppermute | solution.py:312
  40.3 37.4 %collective-permute-start.8 = (f32[128,1152]{1,0:T(8,128)S(1)}, f32[128,1152]{1,0:T(8,128)S(1)}, u32[]{:S(2)}, u32[]{:S(2)}) collective-permute-start(f32[128,1152]{1,0:T(8,128)S(1)} %get-tuple-element.35), channel_id=1, source_target_pairs={{0,8},{16,24},{1,9},{17,25},{2,10},{18,26},{3,11},{19,27},{4,12},{... | collective-permute-start | bytes 1769480 | tf_op jit(solution)/shard_map/ppermute | solution.py:371
  51.5 26.2 %collective-permute-start.10 = (f32[128,1152]{1,0:T(8,128)S(1)}, f32[128,1152]{1,0:T(8,128)S(1)}, u32[]{:S(2)}, u32[]{:S(2)}) collective-permute-start(f32[128,1152]{1,0:T(8,128)S(1)} %collective-permute-done.9.refs_1_), channel_id=1, source_target_pairs={{0,8},{8,0},{16,24},{24,16},{1,9},{9,1},{17,25},{25,17},{2,10},{10... | collective-permute-start | bytes 1769480 | tf_op jit(solution)/shard_map/ppermute | solution.py:377
  53.7 12.7 %collective-permute-start.17 = (f32[512,128]{1,0:T(8,128)S(1)}, f32[512,128]{1,0:T(8,128)S(1)}, u32[]{:S(2)}, u32[]{:S(2)}) collective-permute-start(f32[512,128]{1,0:T(8,128)S(1)} %get-tuple-element.50), channel_id=1, source_target_pairs={{0,4},{1,5},{2,6},{3,7},{4,0},{5,1},{6,2},{7,3},{8,12},{9,13},{10,... | collective-permute-start | bytes 786440 | tf_op jit(solution)/shard_map/ppermute | solution.py:312
  55.8 22.0 %collective-permute-start.11 = (f32[1024,128]{1,0:T(8,128)S(1)}, f32[1024,128]{1,0:T(8,128)S(1)}, u32[]{:S(2)}, u32[]{:S(2)}) collective-permute-start(f32[1024,128]{1,0:T(8,128)S(1)} %get-tuple-element.36), channel_id=1, source_target_pairs={{0,8},{16,24},{1,9},{17,25},{2,10},{18,26},{3,11},{19,27},{4,12},{... | collective-permute-start | bytes 1572872 | tf_op jit(solution)/shard_map/ppermute | solution.py:370
  58.4 19.4 %collective-permute-start.14 = (f32[1024,128]{1,0:T(8,128)S(1)}, f32[1024,128]{1,0:T(8,128)S(1)}, u32[]{:S(2)}, u32[]{:S(2)}) collective-permute-start(f32[1024,128]{1,0:T(8,128)S(1)} %get-tuple-element.37.refs_4_), channel_id=1, source_target_pairs={{0,8},{8,0},{16,24},{24,16},{1,9},{9,1},{17,25},{25,17},{2,10},{10... | collective-permute-start | bytes 1572872 | tf_op jit(solution)/shard_map/ppermute | solution.py:376
  66.4 9.5 %collective-permute-start.15 = (f32[512,128]{1,0:T(8,128)S(1)}, f32[512,128]{1,0:T(8,128)S(1)}, u32[]{:S(2)}, u32[]{:S(2)}) collective-permute-start(f32[512,128]{1,0:T(8,128)S(1)} %get-tuple-element.51), channel_id=1, source_target_pairs={{0,2},{1,3},{2,4},{3,5},{4,6},{5,7},{6,0},{7,1},{8,10},{9,11},{10,... | collective-permute-start | bytes 786440 | tf_op jit(solution)/shard_map/ppermute | solution.py:312
  83.8 22.7 %collective-permute-start.20 = (f32[512,128]{1,0:T(8,128)S(1)}, f32[512,128]{1,0:T(8,128)S(1)}, u32[]{:S(2)}, u32[]{:S(2)}) collective-permute-start(f32[512,128]{1,0:T(8,128)S(1)} %shard_map.67), channel_id=1, source_target_pairs={{0,2},{1,3},{2,4},{3,5},{4,6},{5,7},{6,0},{7,1},{8,10},{9,11},{10,... | collective-permute-start | bytes 786440 | tf_op jit(solution)/shard_map/ppermute | solution.py:424
  88.4 23.1 %collective-permute-start.18 = (f32[512,128]{1,0:T(8,128)S(1)}, f32[512,128]{1,0:T(8,128)S(1)}, u32[]{:S(2)}, u32[]{:S(2)}) collective-permute-start(f32[512,128]{1,0:T(8,128)S(1)} %shard_map.65), channel_id=1, source_target_pairs={{0,4},{1,5},{2,6},{3,7},{4,0},{5,1},{6,2},{7,3},{8,12},{9,13},{10,... | collective-permute-start | bytes 786440 | tf_op jit(solution)/shard_map/ppermute | solution.py:424
  99.7 14.7 %collective-permute-start.16 = (f32[512,128]{1,0:T(8,128)S(1)}, f32[512,128]{1,0:T(8,128)S(1)}, u32[]{:S(2)}, u32[]{:S(2)}) collective-permute-start(f32[512,128]{1,0:T(8,128)S(1)} %shard_map.63), channel_id=1, source_target_pairs={{0,6},{1,7},{2,0},{3,1},{4,2},{5,3},{6,4},{7,5},{8,14},{9,15},{10,... | collective-permute-start | bytes 786440 | tf_op jit(solution)/shard_map/ppermute | solution.py:424

commit v2 on v1

--- a/solution.py
+++ b/solution.py
@@ -136,16 +136,19 @@
     pack_ref[:, blocks * length :] = suffix
 
 
-def value_kernel(heads, ring, length, scal, *refs):
-    vs = refs[:ring]
-    vb_ref, vsec_ref = refs[ring:]
+def lay_values(heads, ring, length, scal, ref, store):
     for r in range(ring):
         lane = lax.rem(scal[1] - r + ring, ring)
         for d in range(heads):
             b = lax.rem(scal[0] - d + heads, heads) * ring + lane
-            at = pl.ds(pl.multiple_of(b * length, length), length)
-            vb_ref[at] = vs[r][d].astype(BF16)
-            vsec_ref[at] = vs[r][d]
+            store(pl.ds(pl.multiple_of(b * length, length), length), ref[r, d].astype(BF16))
+
+
+def value_kernel(heads, ring, length, scal, v_ref, vb_ref):
+    def store(at, x):
+        vb_ref[at] = x
+
+    lay_values(heads, ring, length, scal, v_ref, store)
 
 
 def near_kernel(d, heads, ring, length, width, scal, q_ref, *refs):
@@ -208,7 +211,7 @@
         finish(keys)
 
 
-def prep_kernel(hops, scal, *refs):
+def prep_kernel(hops, heads, ring, length, scal, *refs):
     n = 2 * hops + 1
     packs, values = refs[:n], refs[n : 2 * n]
     kc_ref, vc_ref, got = refs[2 * n :]
@@ -222,7 +225,10 @@
         dst[...] = packs[i][...]
 
     def take_v(dist, i):
-        vc_ref[dist - 1] = values[i][...].astype(BF16)
+        def store(at, x):
+            vc_ref[dist - 1, at] = x
+
+        lay_values(heads, ring, length, scal, values[i], store)
 
     for dist in range(1, n + 1):
         p = dist // 2
@@ -275,10 +281,14 @@
         out_ref[part] = a_s[i] / l_s[i]
 
 
-def join_kernel(heads, scal, *refs):
-    out_ref = refs[heads]
+def join_kernel(heads, group, scal, *refs):
+    out_ref, held = refs[heads:]
+    length = out_ref.shape[0]
     for d in range(heads):
-        out_ref[lax.rem(scal[0] + d, heads)] = refs[d][...].astype(BF16)
+        at = lax.rem(scal[0] + d, heads)
+        for g in range(group):
+            held[at * group + g] = refs[d][g * length : (g + 1) * length]
+    out_ref[...] = jnp.swapaxes(held[...], 0, 1).astype(BF16)
 
 
 def steps(query, key, value, raw_directions, beta_raw_logits):
@@ -308,9 +318,7 @@
         ]
 
     def deal(own):
-        return [own[0]] + [
-            lax.ppermute(own[d], "key", around(d)) for d in range(1, heads)
-        ]
+        return [own[0]] + [lax.ppermute(own[d], "key", around(d)) for d in range(1, heads)]
 
     def gather(x):
         return [x] + [lax.ppermute(x, "key", across(d)) for d in range(1, ring)]
@@ -341,18 +349,15 @@
 
     v_own = jnp.stack(values)
 
-    def arrange(parts):
-        return call(
-            functools.partial(value_kernel, heads, ring, length),
-            (sds((keys, width), BF16), sds((keys, width), F32)),
-            parts,
-            scalars=scal,
-            nbytes=blocks * length * width * 10,
-        )
-
-    v_parts = gather(v_own)
+    v_pair = jnp.stack(gather(v_own))
     km_parts = gather(km)
-    vb, vsec = arrange(v_parts)
+    vb = call(
+        functools.partial(value_kernel, heads, ring, length),
+        sds((keys, width), BF16),
+        [v_pair],
+        scalars=scal,
+        nbytes=keys * width * 6,
+    )
     kmcat, packet = call(
         functools.partial(section_kernel, heads, ring, length),
         (
@@ -367,11 +372,11 @@
 
     pair = [(s, s ^ 1) for s in range(sec_count)]
     rise = [(s, s + 1) for s in range(0, sec_count, 2)]
-    v_far = [lax.ppermute(vsec, "sec", rise)]
+    v_far = [lax.ppermute(v_pair, "sec", rise)]
     k_far = [lax.ppermute(packet, "sec", rise)]
     for p in range(1, hops + 1):
         line = [(s, s + 2 * p) for s in range(sec_count - 2 * p)]
-        v_got = arrange(gather(lax.ppermute(v_own, "sec", line)))[1]
+        v_got = jnp.stack(gather(lax.ppermute(v_own, "sec", line)))
         k_got = lax.ppermute(packet, "sec", line)
         v_far += [v_got, lax.ppermute(v_got, "sec", pair)]
         k_far += [k_got, lax.ppermute(k_got, "sec", pair)]
@@ -392,7 +397,7 @@
     found = {d: near(d) for d in [0] + order[:-1]}
     far_count = 2 * hops + 1
     kc, vc = call(
-        functools.partial(prep_kernel, hops),
+        functools.partial(prep_kernel, hops, heads, ring, length),
         (sds((far_count, 3 * width, keys), BF16), sds((far_count, keys, width), BF16)),
         k_far + v_far,
         scratch=[pltpu.VMEM((width, keys + width), F32)],
@@ -422,14 +427,14 @@
     for d in order:
         piece = far(d)
         back[d] = lax.ppermute(piece, "key", around(-d)) if d else piece
-    joined = call(
-        functools.partial(join_kernel, heads),
-        sds((heads, rows, width), BF16),
+    return call(
+        functools.partial(join_kernel, heads, group),
+        sds((length, q_count, width), BF16),
         back,
+        scratch=[pltpu.VMEM((q_count, length, width), F32)],
         scalars=scal,
         nbytes=heads * rows * width * 6,
     )
-    return jnp.transpose(joined.reshape(q_count, length, width), (1, 0, 2))
 
 
 def solution(mesh):

time: 116 us -> 122 us (1.052)
  the two profiles are of different devices: /device:TPU:11 before, /device:TPU:6 now
where the time goes in v2:
time: 122 us; the launch traced here: 121 us
  waiting for transfers between devices  53.9 us (44%)
  Pallas kernels  34.8 us (29%)
  starting transfers between devices  28.8 us (24%)
  other arithmetic  2.13 us (2%)
    pallas_call x13, Pallas kernels, call(): pl.pallas_call(kernel, out_shape=out_shape, in_specs=specs, out_specs=out...  34.8 us
    ppermute x9, waiting for transfers between devices, deal(): lax.ppermute(own[d], 'key', around(d))  23 us
    ppermute x9, starting transfers between devices, deal(): lax.ppermute(own[d], 'key', around(d))  17.8 us
    ppermute x1, waiting for transfers between devices, steps(): v_got = jnp.stack(gather(lax.ppermute(v_own, 'sec', line)))  17.4 us
    ppermute x3, waiting for transfers between devices, steps(): back[d] = lax.ppermute(piece, 'key', around(-d)) if d else piece  7.93 us
    ppermute x3, waiting for transfers between devices, gather(): return [x] + [lax.ppermute(x, 'key', across(d)) for d in range(1, ring)]  5.52 us
    ppermute x3, starting transfers between devices, steps(): back[d] = lax.ppermute(piece, 'key', around(-d)) if d else piece  4 us
  transfers between devices with their start and end apart: 21, of which 9 were waited for; matrix products, arithmetic and copies ran while one was open for 1% of the time, Pallas kernels for 20%

profile of v2, /device:TPU:6, one launch (start us, length us, event | category | flops | bytes accessed | tf_op | source)
XLA Modules:
  0.0 120.7 jit_solution(3962800779713259059)
XLA Ops:
  2.3 2.7 %collective-permute-start.1 = (f32[264,128]{1,0:T(8,128)S(1)}, f32[264,128]{1,0:T(8,128)S(1)}, u32[]{:S(2)}, u32[]{:S(2)}) collective-permute-start(f32[264,128]{1,0:T(8,128)S(1)} %bitcast.45), channel_id=1, source_target_pairs={{0,4},{1,5},{2,6},{3,7},{4,0},{5,1},{6,2},{7,3},{8,12},{9,13},{10,... | collective-permute-start | bytes 405512 | tf_op jit(solution)/shard_map/ppermute | solution.py:321
  7.1 6.6 %collective-permute-done.1.refs_2_ = f32[264,128]{1,0:T(8,128)S(1)} collective-permute-done((f32[264,128]{1,0:T(8,128)S(1)}, f32[264,128]{1,0:T(8,128)S(1)}, u32[]{:S(2)}, u32[]{:S(2)}) %collective-permute-start.1) | collective-permute-done | bytes 135200 | tf_op jit(solution)/shard_map/ppermute | solution.py:321
  13.7 1.8 %collective-permute-done.refs_1_ = f32[264,128]{1,0:T(8,128)S(1)} collective-permute-done((f32[264,128]{1,0:T(8,128)S(1)}, f32[264,128]{1,0:T(8,128)S(1)}, u32[]{:S(2)}, u32[]{:S(2)}) %collective-permute-start) | collective-permute-done | bytes 135200 | tf_op jit(solution)/shard_map/ppermute | solution.py:321
  15.5 4.3 %shard_map.55 = (f32[4,128,256]{2,1,0:T(8,128)S(1)}, bf16[4,256,256]{2,1,0:T(8,128)(2,1)S(1)}, bf16[4,384,256]{2,1,0:T(8,128)(2,1)S(1)}) custom-call(s32[3]{0:T(128)S(1)} %pad_add_fusion.scal, f32[264,128]{1,0:T(8,128)S(1)} %bitcast.37, f32[264,128]{1,0:T(8,128)S(1)} %collective-permute-done.refs_1_, f32[264,128]{1,0:T(8,128)S(1)} %collective-permute-done.1.refs_2_, ...), custom_call_target="tpu_custom_call" | custom-call | flops 1006632960 | bytes 2621440 | tf_op jit(solution)/shard_map/pallas_call | solution.py:49
  20.7 2.8 %collective-permute-start.6 = (f32[128,128]{1,0:T(8,128)S(1)}, f32[128,128]{1,0:T(8,128)S(1)}, u32[]{:S(2)}, u32[]{:S(2)}) collective-permute-start(f32[128,128]{1,0:T(8,128)S(1)} %bitcast.51), channel_id=1, source_target_pairs={{0,6},{1,7},{2,0},{3,1},{4,2},{5,3},{6,4},{7,5},{8,14},{9,15},{10,... | collective-permute-start | bytes 196616 | tf_op jit(solution)/shard_map/ppermute | solution.py:321
  23.5 1.8 %collective-permute-start.5 = (f32[128,128]{1,0:T(8,128)S(1)}, f32[128,128]{1,0:T(8,128)S(1)}, u32[]{:S(2)}, u32[]{:S(2)}) collective-permute-start(f32[128,128]{1,0:T(8,128)S(1)} %bitcast.50), channel_id=1, source_target_pairs={{0,4},{1,5},{2,6},{3,7},{4,0},{5,1},{6,2},{7,3},{8,12},{9,13},{10,... | collective-permute-start | bytes 196616 | tf_op jit(solution)/shard_map/ppermute | solution.py:321
  25.2 1.9 %collective-permute-start.4 = (f32[128,128]{1,0:T(8,128)S(1)}, f32[128,128]{1,0:T(8,128)S(1)}, u32[]{:S(2)}, u32[]{:S(2)}) collective-permute-start(f32[128,128]{1,0:T(8,128)S(1)} %bitcast.49), channel_id=1, source_target_pairs={{0,2},{1,3},{2,4},{3,5},{4,6},{5,7},{6,0},{7,1},{8,10},{9,11},{10,... | collective-permute-start | bytes 196616 | tf_op jit(solution)/shard_map/ppermute | solution.py:321
  27.2 5.5 %collective-permute-done.3.refs_1_ = f32[4,128,256]{2,1,0:T(8,128)S(1)} collective-permute-done((f32[4,128,256]{2,1,0:T(8,128)S(1)}, f32[4,128,256]{2,1,0:T(8,128)S(1)}, u32[]{:S(2)}, u32[]{:S(2)}) %collective-permute-start.3) | collective-permute-done | bytes 524320 | tf_op jit(solution)/shard_map/ppermute | solution.py:324
  32.7 2.1 %shard_map.56 = (bf16[8,384,256]{2,1,0:T(8,128)(2,1)S(1)}, f32[128,1152]{1,0:T(8,128)S(1)}) custom-call(s32[3]{0:T(128)S(1)} %pad_add_fusion.scal, f32[4,128,256]{2,1,0:T(8,128)S(1)} %get-tuple-element.26.refs_0_, f32[4,128,256]{2,1,0:T(8,128)S(1)} %collective-permute-done.3.refs_1_), custom_call_target="tpu_custom_call" | custom-call | flops 201326592 | bytes 4194304 | tf_op jit(solution)/shard_map/pallas_call | solution.py:49
  38.2 17.4 %collective-permute-done.12 = f32[4,128,128]{2,1,0:T(8,128)S(1)} collective-permute-done((f32[4,128,128]{2,1,0:T(8,128)S(1)}, f32[4,128,128]{2,1,0:T(8,128)S(1)}, u32[]{:S(2)}, u32[]{:S(2)}) %collective-permute-start.12) | collective-permute-done | bytes 262176 | tf_op jit(solution)/shard_map/ppermute | solution.py:379
  56.2 4.3 %collective-permute-start.19 = (f32[512,128]{1,0:T(8,128)S(1)}, f32[512,128]{1,0:T(8,128)S(1)}, u32[]{:S(2)}, u32[]{:S(2)}) collective-permute-start(f32[512,128]{1,0:T(8,128)S(1)} %get-tuple-element.43), channel_id=1, source_target_pairs={{0,6},{1,7},{2,0},{3,1},{4,2},{5,3},{6,4},{7,5},{8,14},{9,15},{10,... | collective-permute-start | bytes 786440 | tf_op jit(solution)/shard_map/ppermute | solution.py:321
  60.5 2.4 %collective-permute-start.17 = (f32[512,128]{1,0:T(8,128)S(1)}, f32[512,128]{1,0:T(8,128)S(1)}, u32[]{:S(2)}, u32[]{:S(2)}) collective-permute-start(f32[512,128]{1,0:T(8,128)S(1)} %get-tuple-element.44), channel_id=1, source_target_pairs={{0,4},{1,5},{2,6},{3,7},{4,0},{5,1},{6,2},{7,3},{8,12},{9,13},{10,... | collective-permute-start | bytes 786440 | tf_op jit(solution)/shard_map/ppermute | solution.py:321
  66.8 11.7 %collective-permute-done.17.q_ref = f32[512,128]{1,0:T(8,128)S(1)} collective-permute-done((f32[512,128]{1,0:T(8,128)S(1)}, f32[512,128]{1,0:T(8,128)S(1)}, u32[]{:S(2)}, u32[]{:S(2)}) %collective-permute-start.17) | collective-permute-done | bytes 262176 | tf_op jit(solution)/shard_map/ppermute | solution.py:321
  79.1 2.5 %shard_map.65 = (bf16[512,384]{1,0:T(8,128)(2,1)S(1)}, f32[512,128]{1,0:T(8,128)S(1)}, f32[512,128]{1,0:T(8,128)S(1)}) custom-call(s32[3]{0:T(128)S(1)} %pad_add_fusion.scal, f32[512,128]{1,0:T(8,128)S(1)} %collective-permute-done.19.q_ref, bf16[4,256,256]{2,1,0:T(8,128)(2,1)S(1)} %get-tuple-element.24.refs_0_, ...), custom_call_target="tpu_custom_call" | custom-call | flops 469762048 | bytes 1048576 | tf_op jit(solution)/shard_map/pallas_call | solution.py:49
  81.7 3.3 %shard_map.63 = (bf16[512,384]{1,0:T(8,128)(2,1)S(1)}, f32[512,128]{1,0:T(8,128)S(1)}, f32[512,128]{1,0:T(8,128)S(1)}) custom-call(s32[3]{0:T(128)S(1)} %pad_add_fusion.scal, f32[512,128]{1,0:T(8,128)S(1)} %collective-permute-done.17.q_ref, bf16[4,256,256]{2,1,0:T(8,128)(2,1)S(1)} %get-tuple-element.24.refs_0_, ...), custom_call_target="tpu_custom_call" | custom-call | flops 469762048 | bytes 1048576 | tf_op jit(solution)/shard_map/pallas_call | solution.py:49
  86.7 3.8 %shard_map.61 = (bf16[512,384]{1,0:T(8,128)(2,1)S(1)}, f32[512,128]{1,0:T(8,128)S(1)}, f32[512,128]{1,0:T(8,128)S(1)}) custom-call(s32[3]{0:T(128)S(1)} %pad_add_fusion.scal, f32[512,128]{1,0:T(8,128)S(1)} %collective-permute-done.15.q_ref, bf16[4,256,256]{2,1,0:T(8,128)(2,1)S(1)} %get-tuple-element.24.refs_0_, ...), custom_call_target="tpu_custom_call" | custom-call | flops 469762048 | bytes 1048576 | tf_op jit(solution)/shard_map/pallas_call | solution.py:49
  92.2 3.2 %shard_map.66 = f32[512,128]{1,0:T(8,128)S(1)} custom-call(s32[3]{0:T(128)S(1)} %pad_add_fusion.scal, bf16[512,384]{1,0:T(8,128)(2,1)S(1)} %get-tuple-element.40.q_ref, f32[512,128]{1,0:T(8,128)S(1)} %get-tuple-element.41.ml_ref, f32[512,128]{1,0:T(8,128)S(1)} %get-tuple-element.42.acc_ref, bf16[3,384,1024]{2,1,0:T(8,128)(2,1)S(1)} %get-tuple-element.32.k_ref, ...), custom_call_target="tpu_custom_call" | custom-call | flops 1610612736 | bytes 4456448 | tf_op jit(solution)/shard_map/pallas_call | solution.py:49
  95.5 3.2 %shard_map.64 = f32[512,128]{1,0:T(8,128)S(1)} custom-call(s32[3]{0:T(128)S(1)} %pad_add_fusion.scal, bf16[512,384]{1,0:T(8,128)(2,1)S(1)} %get-tuple-element.37.q_ref, f32[512,128]{1,0:T(8,128)S(1)} %get-tuple-element.38.ml_ref, f32[512,128]{1,0:T(8,128)S(1)} %get-tuple-element.39.acc_ref, bf16[3,384,1024]{2,1,0:T(8,128)(2,1)S(1)} %get-tuple-element.32.k_ref, ...), custom_call_target="tpu_custom_call" | custom-call | flops 1610612736 | bytes 4456448 | tf_op jit(solution)/shard_map/pallas_call | solution.py:49
  99.8 3.2 %shard_map.62 = f32[512,128]{1,0:T(8,128)S(1)} custom-call(s32[3]{0:T(128)S(1)} %pad_add_fusion.scal, bf16[512,384]{1,0:T(8,128)(2,1)S(1)} %get-tuple-element.34.q_ref, f32[512,128]{1,0:T(8,128)S(1)} %get-tuple-element.35.ml_ref, f32[512,128]{1,0:T(8,128)S(1)} %get-tuple-element.36.acc_ref, bf16[3,384,1024]{2,1,0:T(8,128)(2,1)S(1)} %get-tuple-element.32.k_ref, ...), custom_call_target="tpu_custom_call" | custom-call | flops 1610612736 | bytes 4456448 | tf_op jit(solution)/shard_map/pallas_call | solution.py:49
  103.0 2.9 %collective-permute-start.16 = (f32[512,128]{1,0:T(8,128)S(1)}, f32[512,128]{1,0:T(8,128)S(1)}, u32[]{:S(2)}, u32[]{:S(2)}) collective-permute-start(f32[512,128]{1,0:T(8,128)S(1)} %shard_map.62), channel_id=1, source_target_pairs={{0,6},{1,7},{2,0},{3,1},{4,2},{5,3},{6,4},{7,5},{8,14},{9,15},{10,... | collective-permute-start | bytes 786440 | tf_op jit(solution)/shard_map/ppermute | solution.py:429
  105.9 2.0 %shard_map.58 = (bf16[512,384]{1,0:T(8,128)(2,1)S(1)}, f32[512,128]{1,0:T(8,128)S(1)}, f32[512,128]{1,0:T(8,128)S(1)}) custom-call(s32[3]{0:T(128)S(1)} %pad_add_fusion.scal, f32[512,128]{1,0:T(8,128)S(1)} %get-tuple-element.46.q_ref, bf16[4,256,256]{2,1,0:T(8,128)(2,1)S(1)} %get-tuple-element.24.refs_0_, ...), custom_call_target="tpu_custom_call" | custom-call | flops 469762048 | bytes 1048576 | tf_op jit(solution)/shard_map/pallas_call | solution.py:49
  107.9 3.2 %shard_map.60.refs_0_ = f32[512,128]{1,0:T(8,128)S(1)} custom-call(s32[3]{0:T(128)S(1)} %pad_add_fusion.scal, bf16[512,384]{1,0:T(8,128)(2,1)S(1)} %get-tuple-element.28.q_ref, f32[512,128]{1,0:T(8,128)S(1)} %get-tuple-element.29.ml_ref, f32[512,128]{1,0:T(8,128)S(1)} %get-tuple-element.30.acc_ref, bf16[3,384,1024]{2,1,0:T(8,128)(2,1)S(1)} %get-tuple-element.32.k_ref, ...), custom_call_target="tpu_custom_call" | custom-call | flops 1610612736 | bytes 4456448 | tf_op jit(solution)/shard_map/pallas_call | solution.py:49
  111.2 3.8 %collective-permute-done.18.refs_2_ = f32[512,128]{1,0:T(8,128)S(1)} collective-permute-done((f32[512,128]{1,0:T(8,128)S(1)}, f32[512,128]{1,0:T(8,128)S(1)}, u32[]{:S(2)}, u32[]{:S(2)}) %collective-permute-start.18) | collective-permute-done | bytes 262176 | tf_op jit(solution)/shard_map/ppermute | solution.py:429
  115.0 4.1 %collective-permute-done.16.refs_1_ = f32[512,128]{1,0:T(8,128)S(1)} collective-permute-done((f32[512,128]{1,0:T(8,128)S(1)}, f32[512,128]{1,0:T(8,128)S(1)}, u32[]{:S(2)}, u32[]{:S(2)}) %collective-permute-start.16) | collective-permute-done | bytes 262176 | tf_op jit(solution)/shard_map/ppermute | solution.py:429
  (46 shorter events, 19.6 us)
Async XLA Ops:
  1.8 18.6 %copy-start.1 = (bf16[128,4,128]{2,1,0:T(4,128)(2,1)S(1)}, bf16[128,4,128]{2,1,0:T(4,128)(2,1)}, u32[]{:S(2)}) copy-start(bf16[128,4,128]{2,1,0:T(4,128)(2,1)} %param.7) | copy-start | bytes 393220
  2.3 11.4 %collective-permute-start.1 = (f32[264,128]{1,0:T(8,128)S(1)}, f32[264,128]{1,0:T(8,128)S(1)}, u32[]{:S(2)}, u32[]{:S(2)}) collective-permute-start(f32[264,128]{1,0:T(8,128)S(1)} %bitcast.45), channel_id=1, source_target_pairs={{0,4},{1,5},{2,6},{3,7},{4,0},{5,1},{6,2},{7,3},{8,12},{9,13},{10,... | collective-permute-start | bytes 405512 | tf_op jit(solution)/shard_map/ppermute | solution.py:321
  5.0 8.7 %collective-permute-start.2 = (f32[264,128]{1,0:T(8,128)S(1)}, f32[264,128]{1,0:T(8,128)S(1)}, u32[]{:S(2)}, u32[]{:S(2)}) collective-permute-start(f32[264,128]{1,0:T(8,128)S(1)} %bitcast.44), channel_id=1, source_target_pairs={{0,6},{1,7},{2,0},{3,1},{4,2},{5,3},{6,4},{7,5},{8,14},{9,15},{10,... | collective-permute-start | bytes 405512 | tf_op jit(solution)/shard_map/ppermute | solution.py:321
  6.3 9.2 %collective-permute-start = (f32[264,128]{1,0:T(8,128)S(1)}, f32[264,128]{1,0:T(8,128)S(1)}, u32[]{:S(2)}, u32[]{:S(2)}) collective-permute-start(f32[264,128]{1,0:T(8,128)S(1)} %bitcast.43), channel_id=1, source_target_pairs={{0,2},{1,3},{2,4},{3,5},{4,6},{5,7},{6,0},{7,1},{8,10},{9,11},{10,... | collective-permute-start | bytes 405512 | tf_op jit(solution)/shard_map/ppermute | solution.py:321
  15.5 22.5 %copy-start = (bf16[128,16,128]{2,1,0:T(8,128)(2,1)S(1)}, bf16[128,16,128]{2,1,0:T(8,128)(2,1)}, u32[]{:S(2)}) copy-start(bf16[128,16,128]{2,1,0:T(8,128)(2,1)} %param.5) | copy-start | bytes 1572868
  19.9 12.8 %collective-permute-start.3 = (f32[4,128,256]{2,1,0:T(8,128)S(1)}, f32[4,128,256]{2,1,0:T(8,128)S(1)}, u32[]{:S(2)}, u32[]{:S(2)}) collective-permute-start(f32[4,128,256]{2,1,0:T(8,128)S(1)} %get-tuple-element.26.refs_0_), channel_id=1, source_target_pairs={{0,1},{1,0},{2,3},{3,2},{4,5},{5,4},{6,7},{7,6},{8,9},{9,8},{10,11... | collective-permute-start | bytes 1572872 | tf_op jit(solution)/shard_map/ppermute | solution.py:324
  20.7 15.4 %collective-permute-start.6 = (f32[128,128]{1,0:T(8,128)S(1)}, f32[128,128]{1,0:T(8,128)S(1)}, u32[]{:S(2)}, u32[]{:S(2)}) collective-permute-start(f32[128,128]{1,0:T(8,128)S(1)} %bitcast.51), channel_id=1, source_target_pairs={{0,6},{1,7},{2,0},{3,1},{4,2},{5,3},{6,4},{7,5},{8,14},{9,15},{10,... | collective-permute-start | bytes 196616 | tf_op jit(solution)/shard_map/ppermute | solution.py:321
  23.5 12.6 %collective-permute-start.5 = (f32[128,128]{1,0:T(8,128)S(1)}, f32[128,128]{1,0:T(8,128)S(1)}, u32[]{:S(2)}, u32[]{:S(2)}) collective-permute-start(f32[128,128]{1,0:T(8,128)S(1)} %bitcast.50), channel_id=1, source_target_pairs={{0,4},{1,5},{2,6},{3,7},{4,0},{5,1},{6,2},{7,3},{8,12},{9,13},{10,... | collective-permute-start | bytes 196616 | tf_op jit(solution)/shard_map/ppermute | solution.py:321
  25.2 10.9 %collective-permute-start.4 = (f32[128,128]{1,0:T(8,128)S(1)}, f32[128,128]{1,0:T(8,128)S(1)}, u32[]{:S(2)}, u32[]{:S(2)}) collective-permute-start(f32[128,128]{1,0:T(8,128)S(1)} %bitcast.49), channel_id=1, source_target_pairs={{0,2},{1,3},{2,4},{3,5},{4,6},{5,7},{6,0},{7,1},{8,10},{9,11},{10,... | collective-permute-start | bytes 196616 | tf_op jit(solution)/shard_map/ppermute | solution.py:321
  34.8 30.8 %collective-permute-start.9 = (f32[128,1152]{1,0:T(8,128)S(1)}, f32[128,1152]{1,0:T(8,128)S(1)}, u32[]{:S(2)}, u32[]{:S(2)}) collective-permute-start(f32[128,1152]{1,0:T(8,128)S(1)} %get-tuple-element.31), channel_id=1, source_target_pairs={{0,16},{8,24},{1,17},{9,25},{2,18},{10,26},{3,19},{11,27},{4,20},{... | collective-permute-start | bytes 1769480 | tf_op jit(solution)/shard_map/ppermute | solution.py:380
  36.2 26.7 %collective-permute-start.7 = (f32[4,128,128]{2,1,0:T(8,128)S(1)}, f32[4,128,128]{2,1,0:T(8,128)S(1)}, u32[]{:S(2)}, u32[]{:S(2)}) collective-permute-start(f32[4,128,128]{2,1,0:T(8,128)S(1)} %get-tuple-element.52), channel_id=1, source_target_pairs={{0,1},{1,0},{2,3},{3,2},{4,5},{5,4},{6,7},{7,6},{8,9},{9,8},{10,11... | collective-permute-start | bytes 786440 | tf_op jit(solution)/shard_map/ppermute | solution.py:324
  36.7 18.8 %collective-permute-start.12 = (f32[4,128,128]{2,1,0:T(8,128)S(1)}, f32[4,128,128]{2,1,0:T(8,128)S(1)}, u32[]{:S(2)}, u32[]{:S(2)}) collective-permute-start(f32[4,128,128]{2,1,0:T(8,128)S(1)} %get-tuple-element.52), channel_id=1, source_target_pairs={{0,16},{8,24},{1,17},{9,25},{2,18},{10,26},{3,19},{11,27},{4,20},{... | collective-permute-start | bytes 786440 | tf_op jit(solution)/shard_map/ppermute | solution.py:379
  55.6 8.7 %collective-permute-start.13 = (f32[4,128,128]{2,1,0:T(8,128)S(1)}, f32[4,128,128]{2,1,0:T(8,128)S(1)}, u32[]{:S(2)}, u32[]{:S(2)}) collective-permute-start(f32[4,128,128]{2,1,0:T(8,128)S(1)} %collective-permute-done.12), channel_id=1, source_target_pairs={{0,1},{1,0},{2,3},{3,2},{4,5},{5,4},{6,7},{7,6},{8,9},{9,8},{10,11... | collective-permute-start | bytes 786440 | tf_op jit(solution)/shard_map/ppermute | solution.py:324
  56.2 10.6 %collective-permute-start.19 = (f32[512,128]{1,0:T(8,128)S(1)}, f32[512,128]{1,0:T(8,128)S(1)}, u32[]{:S(2)}, u32[]{:S(2)}) collective-permute-start(f32[512,128]{1,0:T(8,128)S(1)} %get-tuple-element.43), channel_id=1, source_target_pairs={{0,6},{1,7},{2,0},{3,1},{4,2},{5,3},{6,4},{7,5},{8,14},{9,15},{10,... | collective-permute-start | bytes 786440 | tf_op jit(solution)/shard_map/ppermute | solution.py:321
  60.5 18.0 %collective-permute-start.17 = (f32[512,128]{1,0:T(8,128)S(1)}, f32[512,128]{1,0:T(8,128)S(1)}, u32[]{:S(2)}, u32[]{:S(2)}) collective-permute-start(f32[512,128]{1,0:T(8,128)S(1)} %get-tuple-element.44), channel_id=1, source_target_pairs={{0,4},{1,5},{2,6},{3,7},{4,0},{5,1},{6,2},{7,3},{8,12},{9,13},{10,... | collective-permute-start | bytes 786440 | tf_op jit(solution)/shard_map/ppermute | solution.py:321
  62.9 27.6 %collective-permute-start.11 = (f32[2,4,128,128]{3,2,1,0:T(8,128)S(1)}, f32[2,4,128,128]{3,2,1,0:T(8,128)S(1)}, u32[]{:S(2)}, u32[]{:S(2)}) collective-permute-start(f32[2,4,128,128]{3,2,1,0:T(8,128)S(1)} %pad_maximum_fusion.v_ref), channel_id=1, source_target_pairs={{0,8},{16,24},{1,9},{17,25},{2,10},{18,26},{3,11},{19,27},{4,12},{... | collective-permute-start | bytes 1572872 | tf_op jit(solution)/shard_map/ppermute | solution.py:375
  64.3 26.3 %collective-permute-start.8 = (f32[128,1152]{1,0:T(8,128)S(1)}, f32[128,1152]{1,0:T(8,128)S(1)}, u32[]{:S(2)}, u32[]{:S(2)}) collective-permute-start(f32[128,1152]{1,0:T(8,128)S(1)} %get-tuple-element.31), channel_id=1, source_target_pairs={{0,8},{16,24},{1,9},{17,25},{2,10},{18,26},{3,11},{19,27},{4,12},{... | collective-permute-start | bytes 1769480 | tf_op jit(solution)/shard_map/ppermute | solution.py:376
  65.6 25.0 %collective-permute-start.10 = (f32[128,1152]{1,0:T(8,128)S(1)}, f32[128,1152]{1,0:T(8,128)S(1)}, u32[]{:S(2)}, u32[]{:S(2)}) collective-permute-start(f32[128,1152]{1,0:T(8,128)S(1)} %collective-permute-done.9.refs_1_), channel_id=1, source_target_pairs={{0,8},{8,0},{16,24},{24,16},{1,9},{9,1},{17,25},{25,17},{2,10},{10... | collective-permute-start | bytes 1769480 | tf_op jit(solution)/shard_map/ppermute | solution.py:382
  66.8 23.8 %collective-permute-start.14 = (f32[2,4,128,128]{3,2,1,0:T(8,128)S(1)}, f32[2,4,128,128]{3,2,1,0:T(8,128)S(1)}, u32[]{:S(2)}, u32[]{:S(2)}) collective-permute-start(f32[2,4,128,128]{3,2,1,0:T(8,128)S(1)} %pad_maximum_fusion.1.refs_4_), channel_id=1, source_target_pairs={{0,8},{8,0},{16,24},{24,16},{1,9},{9,1},{17,25},{25,17},{2,10},{10... | collective-permute-start | bytes 1572872 | tf_op jit(solution)/shard_map/ppermute | solution.py:381
  78.5 8.2 %collective-permute-start.15 = (f32[512,128]{1,0:T(8,128)S(1)}, f32[512,128]{1,0:T(8,128)S(1)}, u32[]{:S(2)}, u32[]{:S(2)}) collective-permute-start(f32[512,128]{1,0:T(8,128)S(1)} %get-tuple-element.45), channel_id=1, source_target_pairs={{0,2},{1,3},{2,4},{3,5},{4,6},{5,7},{6,0},{7,1},{8,10},{9,11},{10,... | collective-permute-start | bytes 786440 | tf_op jit(solution)/shard_map/ppermute | solution.py:321
  95.4 15.8 %collective-permute-start.20 = (f32[512,128]{1,0:T(8,128)S(1)}, f32[512,128]{1,0:T(8,128)S(1)}, u32[]{:S(2)}, u32[]{:S(2)}) collective-permute-start(f32[512,128]{1,0:T(8,128)S(1)} %shard_map.66), channel_id=1, source_target_pairs={{0,2},{1,3},{2,4},{3,5},{4,6},{5,7},{6,0},{7,1},{8,10},{9,11},{10,... | collective-permute-start | bytes 786440 | tf_op jit(solution)/shard_map/ppermute | solution.py:429
  98.7 16.3 %collective-permute-start.18 = (f32[512,128]{1,0:T(8,128)S(1)}, f32[512,128]{1,0:T(8,128)S(1)}, u32[]{:S(2)}, u32[]{:S(2)}) collective-permute-start(f32[512,128]{1,0:T(8,128)S(1)} %shard_map.64), channel_id=1, source_target_pairs={{0,4},{1,5},{2,6},{3,7},{4,0},{5,1},{6,2},{7,3},{8,12},{9,13},{10,... | collective-permute-start | bytes 786440 | tf_op jit(solution)/shard_map/ppermute | solution.py:429
  103.0 16.1 %collective-permute-start.16 = (f32[512,128]{1,0:T(8,128)S(1)}, f32[512,128]{1,0:T(8,128)S(1)}, u32[]{:S(2)}, u32[]{:S(2)}) collective-permute-start(f32[512,128]{1,0:T(8,128)S(1)} %shard_map.62), channel_id=1, source_target_pairs={{0,6},{1,7},{2,0},{3,1},{4,2},{5,3},{6,4},{7,5},{8,14},{9,15},{10,... | collective-permute-start | bytes 786440 | tf_op jit(solution)/shard_map/ppermute | solution.py:429

commit v3 on v2

--- a/solution.py
+++ b/solution.py
@@ -36,6 +36,22 @@
 
 def dot_nn(a, b):
     return mm(left_cat(a), right_rows(b))
+
+
+def thirds(x):
+    h = x.astype(BF16)
+    rest = x - h.astype(F32)
+    m = rest.astype(BF16)
+    return h, m, (rest - m.astype(F32)).astype(BF16)
+
+
+def dot_fine(a, b):
+    ah, am, al = thirds(a)
+    bh, bm, bl = thirds(b)
+    return mm(
+        jnp.concatenate([ah, am, al, ah, am, ah], axis=1),
+        jnp.concatenate([bh, bh, bh, bm, bm, bl], axis=0),
+    )
 
 
 def call(kernel, out_shape, args, scratch=(), scalars=None, flops=0, nbytes=0, exps=0):
@@ -78,7 +94,7 @@
         beta = jnp.transpose(jnp.broadcast_to(beta, (length, length)))
         unit = w / jnp.sqrt(jnp.sum(w * w, -1, keepdims=True) + 1e-06)
         across = jnp.transpose(unit)
-        low = jnp.where(strict, beta * dot_nn(unit, across), 0.0)
+        low = jnp.where(strict, beta * dot_fine(unit, across), 0.0)
         units.append(unit)
         turned.append(across)
         betas.append(beta)
@@ -87,15 +103,16 @@
         xs.append(eye - jnp.where(level, low, 0.0))
     size = 2
     while size < length:
-        level = (
-            (rows // (2 * size) == cols // (2 * size))
-            & ((rows // size) % 2 == 1)
-            & ((cols // size) % 2 == 0)
-        )
-        part = [dot_nn(jnp.where(level, lows[d], 0.0), xs[d]) for d in range(heads)]
-        part = [dot_nn(xs[d], part[d]) for d in range(heads)]
-        xs = [xs[d] - part[d] for d in range(heads)]
-        size *= 2
+        step = min(4, length // size)
+        level = (rows // (step * size) == cols // (step * size)) & (rows // size > cols // size)
+        links = [dot_fine(xs[d], jnp.where(level, lows[d], 0.0)) for d in range(heads)]
+        both = [
+            dot_fine(links[d], jnp.concatenate([links[d], xs[d]], axis=1)) for d in range(heads)
+        ]
+        xs = [xs[d] - both[d][:, length:] for d in range(heads)]
+        if step == 4:
+            xs = [xs[d] + dot_fine(both[d][:, :length], xs[d]) for d in range(heads)]
+        size *= step
     for d in range(heads):
         slot = lax.rem(place - d + heads, heads)
         unit, beta, across = units[d], betas[d], turned[d]

time: 122 us -> 122 us (level)
  no operation moved by 1% of the time
where the time goes in v3:
time: 122 us; the launch traced here: 121 us
  waiting for transfers between devices  53.9 us (44%)
  Pallas kernels  34.9 us (29%)
  starting transfers between devices  28.8 us (24%)
  other arithmetic  2.13 us (2%)
    pallas_call x13, Pallas kernels, call(): pl.pallas_call(kernel, out_shape=out_shape, in_specs=specs, out_specs=out...  34.9 us
    ppermute x9, waiting for transfers between devices, deal(): lax.ppermute(own[d], 'key', around(d))  23 us
    ppermute x9, starting transfers between devices, deal(): lax.ppermute(own[d], 'key', around(d))  17.8 us
    ppermute x1, waiting for transfers between devices, steps(): v_got = jnp.stack(gather(lax.ppermute(v_own, 'sec', line)))  17.4 us
    ppermute x3, waiting for transfers between devices, steps(): back[d] = lax.ppermute(piece, 'key', around(-d)) if d else piece  7.94 us
    ppermute x3, waiting for transfers between devices, gather(): return [x] + [lax.ppermute(x, 'key', across(d)) for d in range(1, ring)]  5.52 us
    ppermute x3, starting transfers between devices, steps(): back[d] = lax.ppermute(piece, 'key', around(-d)) if d else piece  4 us
  transfers between devices with their start and end apart: 21, of which 9 were waited for; matrix products, arithmetic and copies ran while one was open for 1% of the time, Pallas kernels for 20%

profile of v3, /device:TPU:6, one launch (start us, length us, event | category | flops | bytes accessed | tf_op | source)
XLA Modules:
  0.0 120.8 jit_solution(500623018993328797)
XLA Ops:
  2.3 2.7 %collective-permute-start.1 = (f32[264,128]{1,0:T(8,128)S(1)}, f32[264,128]{1,0:T(8,128)S(1)}, u32[]{:S(2)}, u32[]{:S(2)}) collective-permute-start(f32[264,128]{1,0:T(8,128)S(1)} %bitcast.45), channel_id=1, source_target_pairs={{0,4},{1,5},{2,6},{3,7},{4,0},{5,1},{6,2},{7,3},{8,12},{9,13},{10,... | collective-permute-start | bytes 405512 | tf_op jit(solution)/shard_map/ppermute | solution.py:338
  7.1 6.6 %collective-permute-done.1.refs_2_ = f32[264,128]{1,0:T(8,128)S(1)} collective-permute-done((f32[264,128]{1,0:T(8,128)S(1)}, f32[264,128]{1,0:T(8,128)S(1)}, u32[]{:S(2)}, u32[]{:S(2)}) %collective-permute-start.1) | collective-permute-done | bytes 135200 | tf_op jit(solution)/shard_map/ppermute | solution.py:338
  13.7 1.8 %collective-permute-done.refs_1_ = f32[264,128]{1,0:T(8,128)S(1)} collective-permute-done((f32[264,128]{1,0:T(8,128)S(1)}, f32[264,128]{1,0:T(8,128)S(1)}, u32[]{:S(2)}, u32[]{:S(2)}) %collective-permute-start) | collective-permute-done | bytes 135200 | tf_op jit(solution)/shard_map/ppermute | solution.py:338
  15.5 4.4 %shard_map.55 = (f32[4,128,256]{2,1,0:T(8,128)S(1)}, bf16[4,256,256]{2,1,0:T(8,128)(2,1)S(1)}, bf16[4,384,256]{2,1,0:T(8,128)(2,1)S(1)}) custom-call(s32[3]{0:T(128)S(1)} %pad_add_fusion.scal, f32[264,128]{1,0:T(8,128)S(1)} %bitcast.37, f32[264,128]{1,0:T(8,128)S(1)} %collective-permute-done.refs_1_, f32[264,128]{1,0:T(8,128)S(1)} %collective-permute-done.1.refs_2_, ...), custom_call_target="tpu_custom_call" | custom-call | flops 1006632960 | bytes 2621440 | tf_op jit(solution)/shard_map/pallas_call | solution.py:65
  20.8 2.8 %collective-permute-start.6 = (f32[128,128]{1,0:T(8,128)S(1)}, f32[128,128]{1,0:T(8,128)S(1)}, u32[]{:S(2)}, u32[]{:S(2)}) collective-permute-start(f32[128,128]{1,0:T(8,128)S(1)} %bitcast.51), channel_id=1, source_target_pairs={{0,6},{1,7},{2,0},{3,1},{4,2},{5,3},{6,4},{7,5},{8,14},{9,15},{10,... | collective-permute-start | bytes 196616 | tf_op jit(solution)/shard_map/ppermute | solution.py:338
  23.5 1.8 %collective-permute-start.5 = (f32[128,128]{1,0:T(8,128)S(1)}, f32[128,128]{1,0:T(8,128)S(1)}, u32[]{:S(2)}, u32[]{:S(2)}) collective-permute-start(f32[128,128]{1,0:T(8,128)S(1)} %bitcast.50), channel_id=1, source_target_pairs={{0,4},{1,5},{2,6},{3,7},{4,0},{5,1},{6,2},{7,3},{8,12},{9,13},{10,... | collective-permute-start | bytes 196616 | tf_op jit(solution)/shard_map/ppermute | solution.py:338
  25.3 1.9 %collective-permute-start.4 = (f32[128,128]{1,0:T(8,128)S(1)}, f32[128,128]{1,0:T(8,128)S(1)}, u32[]{:S(2)}, u32[]{:S(2)}) collective-permute-start(f32[128,128]{1,0:T(8,128)S(1)} %bitcast.49), channel_id=1, source_target_pairs={{0,2},{1,3},{2,4},{3,5},{4,6},{5,7},{6,0},{7,1},{8,10},{9,11},{10,... | collective-permute-start | bytes 196616 | tf_op jit(solution)/shard_map/ppermute | solution.py:338
  27.2 5.5 %collective-permute-done.3.refs_1_ = f32[4,128,256]{2,1,0:T(8,128)S(1)} collective-permute-done((f32[4,128,256]{2,1,0:T(8,128)S(1)}, f32[4,128,256]{2,1,0:T(8,128)S(1)}, u32[]{:S(2)}, u32[]{:S(2)}) %collective-permute-start.3) | collective-permute-done | bytes 524320 | tf_op jit(solution)/shard_map/ppermute | solution.py:341
  32.7 2.1 %shard_map.56 = (bf16[8,384,256]{2,1,0:T(8,128)(2,1)S(1)}, f32[128,1152]{1,0:T(8,128)S(1)}) custom-call(s32[3]{0:T(128)S(1)} %pad_add_fusion.scal, f32[4,128,256]{2,1,0:T(8,128)S(1)} %get-tuple-element.26.refs_0_, f32[4,128,256]{2,1,0:T(8,128)S(1)} %collective-permute-done.3.refs_1_), custom_call_target="tpu_custom_call" | custom-call | flops 201326592 | bytes 4194304 | tf_op jit(solution)/shard_map/pallas_call | solution.py:65
  38.2 17.4 %collective-permute-done.12 = f32[4,128,128]{2,1,0:T(8,128)S(1)} collective-permute-done((f32[4,128,128]{2,1,0:T(8,128)S(1)}, f32[4,128,128]{2,1,0:T(8,128)S(1)}, u32[]{:S(2)}, u32[]{:S(2)}) %collective-permute-start.12) | collective-permute-done | bytes 262176 | tf_op jit(solution)/shard_map/ppermute | solution.py:396
  56.2 4.3 %collective-permute-start.19 = (f32[512,128]{1,0:T(8,128)S(1)}, f32[512,128]{1,0:T(8,128)S(1)}, u32[]{:S(2)}, u32[]{:S(2)}) collective-permute-start(f32[512,128]{1,0:T(8,128)S(1)} %get-tuple-element.43), channel_id=1, source_target_pairs={{0,6},{1,7},{2,0},{3,1},{4,2},{5,3},{6,4},{7,5},{8,14},{9,15},{10,... | collective-permute-start | bytes 786440 | tf_op jit(solution)/shard_map/ppermute | solution.py:338
  60.5 2.4 %collective-permute-start.17 = (f32[512,128]{1,0:T(8,128)S(1)}, f32[512,128]{1,0:T(8,128)S(1)}, u32[]{:S(2)}, u32[]{:S(2)}) collective-permute-start(f32[512,128]{1,0:T(8,128)S(1)} %get-tuple-element.44), channel_id=1, source_target_pairs={{0,4},{1,5},{2,6},{3,7},{4,0},{5,1},{6,2},{7,3},{8,12},{9,13},{10,... | collective-permute-start | bytes 786440 | tf_op jit(solution)/shard_map/ppermute | solution.py:338
  66.8 11.7 %collective-permute-done.17.q_ref = f32[512,128]{1,0:T(8,128)S(1)} collective-permute-done((f32[512,128]{1,0:T(8,128)S(1)}, f32[512,128]{1,0:T(8,128)S(1)}, u32[]{:S(2)}, u32[]{:S(2)}) %collective-permute-start.17) | collective-permute-done | bytes 262176 | tf_op jit(solution)/shard_map/ppermute | solution.py:338
  79.1 2.5 %shard_map.65 = (bf16[512,384]{1,0:T(8,128)(2,1)S(1)}, f32[512,128]{1,0:T(8,128)S(1)}, f32[512,128]{1,0:T(8,128)S(1)}) custom-call(s32[3]{0:T(128)S(1)} %pad_add_fusion.scal, f32[512,128]{1,0:T(8,128)S(1)} %collective-permute-done.19.q_ref, bf16[4,256,256]{2,1,0:T(8,128)(2,1)S(1)} %get-tuple-element.24.refs_0_, ...), custom_call_target="tpu_custom_call" | custom-call | flops 469762048 | bytes 1048576 | tf_op jit(solution)/shard_map/pallas_call | solution.py:65
  81.7 3.3 %shard_map.63 = (bf16[512,384]{1,0:T(8,128)(2,1)S(1)}, f32[512,128]{1,0:T(8,128)S(1)}, f32[512,128]{1,0:T(8,128)S(1)}) custom-call(s32[3]{0:T(128)S(1)} %pad_add_fusion.scal, f32[512,128]{1,0:T(8,128)S(1)} %collective-permute-done.17.q_ref, bf16[4,256,256]{2,1,0:T(8,128)(2,1)S(1)} %get-tuple-element.24.refs_0_, ...), custom_call_target="tpu_custom_call" | custom-call | flops 469762048 | bytes 1048576 | tf_op jit(solution)/shard_map/pallas_call | solution.py:65
  86.7 4.0 %shard_map.61 = (bf16[512,384]{1,0:T(8,128)(2,1)S(1)}, f32[512,128]{1,0:T(8,128)S(1)}, f32[512,128]{1,0:T(8,128)S(1)}) custom-call(s32[3]{0:T(128)S(1)} %pad_add_fusion.scal, f32[512,128]{1,0:T(8,128)S(1)} %collective-permute-done.15.q_ref, bf16[4,256,256]{2,1,0:T(8,128)(2,1)S(1)} %get-tuple-element.24.refs_0_, ...), custom_call_target="tpu_custom_call" | custom-call | flops 469762048 | bytes 1048576 | tf_op jit(solution)/shard_map/pallas_call | solution.py:65
  92.2 3.2 %shard_map.66 = f32[512,128]{1,0:T(8,128)S(1)} custom-call(s32[3]{0:T(128)S(1)} %pad_add_fusion.scal, bf16[512,384]{1,0:T(8,128)(2,1)S(1)} %get-tuple-element.40.q_ref, f32[512,128]{1,0:T(8,128)S(1)} %get-tuple-element.41.ml_ref, f32[512,128]{1,0:T(8,128)S(1)} %get-tuple-element.42.acc_ref, bf16[3,384,1024]{2,1,0:T(8,128)(2,1)S(1)} %get-tuple-element.32.k_ref, ...), custom_call_target="tpu_custom_call" | custom-call | flops 1610612736 | bytes 4456448 | tf_op jit(solution)/shard_map/pallas_call | solution.py:65
  95.5 3.2 %shard_map.64 = f32[512,128]{1,0:T(8,128)S(1)} custom-call(s32[3]{0:T(128)S(1)} %pad_add_fusion.scal, bf16[512,384]{1,0:T(8,128)(2,1)S(1)} %get-tuple-element.37.q_ref, f32[512,128]{1,0:T(8,128)S(1)} %get-tuple-element.38.ml_ref, f32[512,128]{1,0:T(8,128)S(1)} %get-tuple-element.39.acc_ref, bf16[3,384,1024]{2,1,0:T(8,128)(2,1)S(1)} %get-tuple-element.32.k_ref, ...), custom_call_target="tpu_custom_call" | custom-call | flops 1610612736 | bytes 4456448 | tf_op jit(solution)/shard_map/pallas_call | solution.py:65
  99.8 3.2 %shard_map.62 = f32[512,128]{1,0:T(8,128)S(1)} custom-call(s32[3]{0:T(128)S(1)} %pad_add_fusion.scal, bf16[512,384]{1,0:T(8,128)(2,1)S(1)} %get-tuple-element.34.q_ref, f32[512,128]{1,0:T(8,128)S(1)} %get-tuple-element.35.ml_ref, f32[512,128]{1,0:T(8,128)S(1)} %get-tuple-element.36.acc_ref, bf16[3,384,1024]{2,1,0:T(8,128)(2,1)S(1)} %get-tuple-element.32.k_ref, ...), custom_call_target="tpu_custom_call" | custom-call | flops 1610612736 | bytes 4456448 | tf_op jit(solution)/shard_map/pallas_call | solution.py:65
  103.1 2.9 %collective-permute-start.16 = (f32[512,128]{1,0:T(8,128)S(1)}, f32[512,128]{1,0:T(8,128)S(1)}, u32[]{:S(2)}, u32[]{:S(2)}) collective-permute-start(f32[512,128]{1,0:T(8,128)S(1)} %shard_map.62), channel_id=1, source_target_pairs={{0,6},{1,7},{2,0},{3,1},{4,2},{5,3},{6,4},{7,5},{8,14},{9,15},{10,... | collective-permute-start | bytes 786440 | tf_op jit(solution)/shard_map/ppermute | solution.py:446
  105.9 2.0 %shard_map.58 = (bf16[512,384]{1,0:T(8,128)(2,1)S(1)}, f32[512,128]{1,0:T(8,128)S(1)}, f32[512,128]{1,0:T(8,128)S(1)}) custom-call(s32[3]{0:T(128)S(1)} %pad_add_fusion.scal, f32[512,128]{1,0:T(8,128)S(1)} %get-tuple-element.46.q_ref, bf16[4,256,256]{2,1,0:T(8,128)(2,1)S(1)} %get-tuple-element.24.refs_0_, ...), custom_call_target="tpu_custom_call" | custom-call | flops 469762048 | bytes 1048576 | tf_op jit(solution)/shard_map/pallas_call | solution.py:65
  108.0 3.2 %shard_map.60.refs_0_ = f32[512,128]{1,0:T(8,128)S(1)} custom-call(s32[3]{0:T(128)S(1)} %pad_add_fusion.scal, bf16[512,384]{1,0:T(8,128)(2,1)S(1)} %get-tuple-element.28.q_ref, f32[512,128]{1,0:T(8,128)S(1)} %get-tuple-element.29.ml_ref, f32[512,128]{1,0:T(8,128)S(1)} %get-tuple-element.30.acc_ref, bf16[3,384,1024]{2,1,0:T(8,128)(2,1)S(1)} %get-tuple-element.32.k_ref, ...), custom_call_target="tpu_custom_call" | custom-call | flops 1610612736 | bytes 4456448 | tf_op jit(solution)/shard_map/pallas_call | solution.py:65
  111.2 3.8 %collective-permute-done.18.refs_2_ = f32[512,128]{1,0:T(8,128)S(1)} collective-permute-done((f32[512,128]{1,0:T(8,128)S(1)}, f32[512,128]{1,0:T(8,128)S(1)}, u32[]{:S(2)}, u32[]{:S(2)}) %collective-permute-start.18) | collective-permute-done | bytes 262176 | tf_op jit(solution)/shard_map/ppermute | solution.py:446
  115.0 4.1 %collective-permute-done.16.refs_1_ = f32[512,128]{1,0:T(8,128)S(1)} collective-permute-done((f32[512,128]{1,0:T(8,128)S(1)}, f32[512,128]{1,0:T(8,128)S(1)}, u32[]{:S(2)}, u32[]{:S(2)}) %collective-permute-start.16) | collective-permute-done | bytes 262176 | tf_op jit(solution)/shard_map/ppermute | solution.py:446
  (46 shorter events, 19.4 us)
Async XLA Ops:
  1.8 18.7 %copy-start.1 = (bf16[128,4,128]{2,1,0:T(4,128)(2,1)S(1)}, bf16[128,4,128]{2,1,0:T(4,128)(2,1)}, u32[]{:S(2)}) copy-start(bf16[128,4,128]{2,1,0:T(4,128)(2,1)} %param.7) | copy-start | bytes 393220
  2.3 11.4 %collective-permute-start.1 = (f32[264,128]{1,0:T(8,128)S(1)}, f32[264,128]{1,0:T(8,128)S(1)}, u32[]{:S(2)}, u32[]{:S(2)}) collective-permute-start(f32[264,128]{1,0:T(8,128)S(1)} %bitcast.45), channel_id=1, source_target_pairs={{0,4},{1,5},{2,6},{3,7},{4,0},{5,1},{6,2},{7,3},{8,12},{9,13},{10,... | collective-permute-start | bytes 405512 | tf_op jit(solution)/shard_map/ppermute | solution.py:338
  5.0 8.7 %collective-permute-start.2 = (f32[264,128]{1,0:T(8,128)S(1)}, f32[264,128]{1,0:T(8,128)S(1)}, u32[]{:S(2)}, u32[]{:S(2)}) collective-permute-start(f32[264,128]{1,0:T(8,128)S(1)} %bitcast.44), channel_id=1, source_target_pairs={{0,6},{1,7},{2,0},{3,1},{4,2},{5,3},{6,4},{7,5},{8,14},{9,15},{10,... | collective-permute-start | bytes 405512 | tf_op jit(solution)/shard_map/ppermute | solution.py:338
  6.3 9.2 %collective-permute-start = (f32[264,128]{1,0:T(8,128)S(1)}, f32[264,128]{1,0:T(8,128)S(1)}, u32[]{:S(2)}, u32[]{:S(2)}) collective-permute-start(f32[264,128]{1,0:T(8,128)S(1)} %bitcast.43), channel_id=1, source_target_pairs={{0,2},{1,3},{2,4},{3,5},{4,6},{5,7},{6,0},{7,1},{8,10},{9,11},{10,... | collective-permute-start | bytes 405512 | tf_op jit(solution)/shard_map/ppermute | solution.py:338
  15.5 22.5 %copy-start = (bf16[128,16,128]{2,1,0:T(8,128)(2,1)S(1)}, bf16[128,16,128]{2,1,0:T(8,128)(2,1)}, u32[]{:S(2)}) copy-start(bf16[128,16,128]{2,1,0:T(8,128)(2,1)} %param.5) | copy-start | bytes 1572868
  19.9 12.8 %collective-permute-start.3 = (f32[4,128,256]{2,1,0:T(8,128)S(1)}, f32[4,128,256]{2,1,0:T(8,128)S(1)}, u32[]{:S(2)}, u32[]{:S(2)}) collective-permute-start(f32[4,128,256]{2,1,0:T(8,128)S(1)} %get-tuple-element.26.refs_0_), channel_id=1, source_target_pairs={{0,1},{1,0},{2,3},{3,2},{4,5},{5,4},{6,7},{7,6},{8,9},{9,8},{10,11... | collective-permute-start | bytes 1572872 | tf_op jit(solution)/shard_map/ppermute | solution.py:341
  20.8 15.4 %collective-permute-start.6 = (f32[128,128]{1,0:T(8,128)S(1)}, f32[128,128]{1,0:T(8,128)S(1)}, u32[]{:S(2)}, u32[]{:S(2)}) collective-permute-start(f32[128,128]{1,0:T(8,128)S(1)} %bitcast.51), channel_id=1, source_target_pairs={{0,6},{1,7},{2,0},{3,1},{4,2},{5,3},{6,4},{7,5},{8,14},{9,15},{10,... | collective-permute-start | bytes 196616 | tf_op jit(solution)/shard_map/ppermute | solution.py:338
  23.5 12.6 %collective-permute-start.5 = (f32[128,128]{1,0:T(8,128)S(1)}, f32[128,128]{1,0:T(8,128)S(1)}, u32[]{:S(2)}, u32[]{:S(2)}) collective-permute-start(f32[128,128]{1,0:T(8,128)S(1)} %bitcast.50), channel_id=1, source_target_pairs={{0,4},{1,5},{2,6},{3,7},{4,0},{5,1},{6,2},{7,3},{8,12},{9,13},{10,... | collective-permute-start | bytes 196616 | tf_op jit(solution)/shard_map/ppermute | solution.py:338
  25.3 10.9 %collective-permute-start.4 = (f32[128,128]{1,0:T(8,128)S(1)}, f32[128,128]{1,0:T(8,128)S(1)}, u32[]{:S(2)}, u32[]{:S(2)}) collective-permute-start(f32[128,128]{1,0:T(8,128)S(1)} %bitcast.49), channel_id=1, source_target_pairs={{0,2},{1,3},{2,4},{3,5},{4,6},{5,7},{6,0},{7,1},{8,10},{9,11},{10,... | collective-permute-start | bytes 196616 | tf_op jit(solution)/shard_map/ppermute | solution.py:338
  34.8 30.8 %collective-permute-start.9 = (f32[128,1152]{1,0:T(8,128)S(1)}, f32[128,1152]{1,0:T(8,128)S(1)}, u32[]{:S(2)}, u32[]{:S(2)}) collective-permute-start(f32[128,1152]{1,0:T(8,128)S(1)} %get-tuple-element.31), channel_id=1, source_target_pairs={{0,16},{8,24},{1,17},{9,25},{2,18},{10,26},{3,19},{11,27},{4,20},{... | collective-permute-start | bytes 1769480 | tf_op jit(solution)/shard_map/ppermute | solution.py:397
  36.2 26.7 %collective-permute-start.7 = (f32[4,128,128]{2,1,0:T(8,128)S(1)}, f32[4,128,128]{2,1,0:T(8,128)S(1)}, u32[]{:S(2)}, u32[]{:S(2)}) collective-permute-start(f32[4,128,128]{2,1,0:T(8,128)S(1)} %get-tuple-element.52), channel_id=1, source_target_pairs={{0,1},{1,0},{2,3},{3,2},{4,5},{5,4},{6,7},{7,6},{8,9},{9,8},{10,11... | collective-permute-start | bytes 786440 | tf_op jit(solution)/shard_map/ppermute | solution.py:341
  36.8 18.9 %collective-permute-start.12 = (f32[4,128,128]{2,1,0:T(8,128)S(1)}, f32[4,128,128]{2,1,0:T(8,128)S(1)}, u32[]{:S(2)}, u32[]{:S(2)}) collective-permute-start(f32[4,128,128]{2,1,0:T(8,128)S(1)} %get-tuple-element.52), channel_id=1, source_target_pairs={{0,16},{8,24},{1,17},{9,25},{2,18},{10,26},{3,19},{11,27},{4,20},{... | collective-permute-start | bytes 786440 | tf_op jit(solution)/shard_map/ppermute | solution.py:396
  55.6 8.6 %collective-permute-start.13 = (f32[4,128,128]{2,1,0:T(8,128)S(1)}, f32[4,128,128]{2,1,0:T(8,128)S(1)}, u32[]{:S(2)}, u32[]{:S(2)}) collective-permute-start(f32[4,128,128]{2,1,0:T(8,128)S(1)} %collective-permute-done.12), channel_id=1, source_target_pairs={{0,1},{1,0},{2,3},{3,2},{4,5},{5,4},{6,7},{7,6},{8,9},{9,8},{10,11... | collective-permute-start | bytes 786440 | tf_op jit(solution)/shard_map/ppermute | solution.py:341
  56.2 10.6 %collective-permute-start.19 = (f32[512,128]{1,0:T(8,128)S(1)}, f32[512,128]{1,0:T(8,128)S(1)}, u32[]{:S(2)}, u32[]{:S(2)}) collective-permute-start(f32[512,128]{1,0:T(8,128)S(1)} %get-tuple-element.43), channel_id=1, source_target_pairs={{0,6},{1,7},{2,0},{3,1},{4,2},{5,3},{6,4},{7,5},{8,14},{9,15},{10,... | collective-permute-start | bytes 786440 | tf_op jit(solution)/shard_map/ppermute | solution.py:338
  60.5 18.0 %collective-permute-start.17 = (f32[512,128]{1,0:T(8,128)S(1)}, f32[512,128]{1,0:T(8,128)S(1)}, u32[]{:S(2)}, u32[]{:S(2)}) collective-permute-start(f32[512,128]{1,0:T(8,128)S(1)} %get-tuple-element.44), channel_id=1, source_target_pairs={{0,4},{1,5},{2,6},{3,7},{4,0},{5,1},{6,2},{7,3},{8,12},{9,13},{10,... | collective-permute-start | bytes 786440 | tf_op jit(solution)/shard_map/ppermute | solution.py:338
  62.9 27.8 %collective-permute-start.11 = (f32[2,4,128,128]{3,2,1,0:T(8,128)S(1)}, f32[2,4,128,128]{3,2,1,0:T(8,128)S(1)}, u32[]{:S(2)}, u32[]{:S(2)}) collective-permute-start(f32[2,4,128,128]{3,2,1,0:T(8,128)S(1)} %pad_maximum_fusion.v_ref), channel_id=1, source_target_pairs={{0,8},{16,24},{1,9},{17,25},{2,10},{18,26},{3,11},{19,27},{4,12},{... | collective-permute-start | bytes 1572872 | tf_op jit(solution)/shard_map/ppermute | solution.py:392
  64.3 26.5 %collective-permute-start.8 = (f32[128,1152]{1,0:T(8,128)S(1)}, f32[128,1152]{1,0:T(8,128)S(1)}, u32[]{:S(2)}, u32[]{:S(2)}) collective-permute-start(f32[128,1152]{1,0:T(8,128)S(1)} %get-tuple-element.31), channel_id=1, source_target_pairs={{0,8},{16,24},{1,9},{17,25},{2,10},{18,26},{3,11},{19,27},{4,12},{... | collective-permute-start | bytes 1769480 | tf_op jit(solution)/shard_map/ppermute | solution.py:393
  65.6 25.2 %collective-permute-start.10 = (f32[128,1152]{1,0:T(8,128)S(1)}, f32[128,1152]{1,0:T(8,128)S(1)}, u32[]{:S(2)}, u32[]{:S(2)}) collective-permute-start(f32[128,1152]{1,0:T(8,128)S(1)} %collective-permute-done.9.refs_1_), channel_id=1, source_target_pairs={{0,8},{8,0},{16,24},{24,16},{1,9},{9,1},{17,25},{25,17},{2,10},{10... | collective-permute-start | bytes 1769480 | tf_op jit(solution)/shard_map/ppermute | solution.py:399
  66.8 23.9 %collective-permute-start.14 = (f32[2,4,128,128]{3,2,1,0:T(8,128)S(1)}, f32[2,4,128,128]{3,2,1,0:T(8,128)S(1)}, u32[]{:S(2)}, u32[]{:S(2)}) collective-permute-start(f32[2,4,128,128]{3,2,1,0:T(8,128)S(1)} %pad_maximum_fusion.1.refs_4_), channel_id=1, source_target_pairs={{0,8},{8,0},{16,24},{24,16},{1,9},{9,1},{17,25},{25,17},{2,10},{10... | collective-permute-start | bytes 1572872 | tf_op jit(solution)/shard_map/ppermute | solution.py:398
  78.5 8.2 %collective-permute-start.15 = (f32[512,128]{1,0:T(8,128)S(1)}, f32[512,128]{1,0:T(8,128)S(1)}, u32[]{:S(2)}, u32[]{:S(2)}) collective-permute-start(f32[512,128]{1,0:T(8,128)S(1)} %get-tuple-element.45), channel_id=1, source_target_pairs={{0,2},{1,3},{2,4},{3,5},{4,6},{5,7},{6,0},{7,1},{8,10},{9,11},{10,... | collective-permute-start | bytes 786440 | tf_op jit(solution)/shard_map/ppermute | solution.py:338
  95.4 15.8 %collective-permute-start.20 = (f32[512,128]{1,0:T(8,128)S(1)}, f32[512,128]{1,0:T(8,128)S(1)}, u32[]{:S(2)}, u32[]{:S(2)}) collective-permute-start(f32[512,128]{1,0:T(8,128)S(1)} %shard_map.66), channel_id=1, source_target_pairs={{0,2},{1,3},{2,4},{3,5},{4,6},{5,7},{6,0},{7,1},{8,10},{9,11},{10,... | collective-permute-start | bytes 786440 | tf_op jit(solution)/shard_map/ppermute | solution.py:446
  98.8 16.3 %collective-permute-start.18 = (f32[512,128]{1,0:T(8,128)S(1)}, f32[512,128]{1,0:T(8,128)S(1)}, u32[]{:S(2)}, u32[]{:S(2)}) collective-permute-start(f32[512,128]{1,0:T(8,128)S(1)} %shard_map.64), channel_id=1, source_target_pairs={{0,4},{1,5},{2,6},{3,7},{4,0},{5,1},{6,2},{7,3},{8,12},{9,13},{10,... | collective-permute-start | bytes 786440 | tf_op jit(solution)/shard_map/ppermute | solution.py:446
  103.1 16.1 %collective-permute-start.16 = (f32[512,128]{1,0:T(8,128)S(1)}, f32[512,128]{1,0:T(8,128)S(1)}, u32[]{:S(2)}, u32[]{:S(2)}) collective-permute-start(f32[512,128]{1,0:T(8,128)S(1)} %shard_map.62), channel_id=1, source_target_pairs={{0,6},{1,7},{2,0},{3,1},{4,2},{5,3},{6,4},{7,5},{8,14},{9,15},{10,... | collective-permute-start | bytes 786440 | tf_op jit(solution)/shard_map/ppermute | solution.py:446
